TPU v7x, 32 devices: a whole 2x2x4 slice. The times are simulated.
32 devices in a mesh: ctx: 4 (over y, x), head: 8 (over z, core).
Axes of the slice: x: 2, y: 2, z: 4, core: 2. Of those that a mesh axis runs over, the one named last changes fastest.
Arguments:
- queries: bfloat16 [4096, 8192], P('ctx', 'head'), may hold values from -12 to 12
- key_heads: bfloat16 [1024, 4096], P(None, 'ctx'), may hold values from -6 to 6
- value_heads: bfloat16 [1024, 4096], P(None, 'ctx'), may hold values from -6 to 6
- out_weight: bfloat16 [8192, 8192], P('head'), may hold values from -0.09375 to 0.09375
- block_order: int32 [8], replicated, may hold values from 0 to 7, each once
- doc_ids: int32 [4096], replicated, may hold values from 0 to 5, never falling along the last dimension, each value on 1 to 1024 neighbouring positions
Outputs:
- projected: bfloat16 [4096, 8192], P('ctx', 'head')
Inputs may be any that keep to these rules, and one draw needn't show every extreme that they name: Layout slot j (rows j * 512 to (j + 1) * 512 - 1 of queries and projected, the same columns of key_heads and value_heads) holds block block_order[j] of the sequence; each of 0 to 7 appears once. `doc_ids`: ids never fall along the sequence; every id is used; each document holds 1 to 1024 tokens and one holds exactly 1024.
All inputs are finite; a program needn't handle non-finite values.
Results may differ from a plain program's by a relative error of at most 0.014.
Values may be sent and summed in bfloat16 or wider, within the bound.
No kernel may reach another device: no remote copies, remote signals or barrier semaphores. Data moves between devices by JAX's collectives and lax.ppermute only.
A program may use at most 192 MiB of HBM per device.

v0:
```python
import jax
import jax.numpy as jnp
from jax import lax
from jax.sharding import PartitionSpec as P

KVH = 8
HD = 128


floor_score = -1e30


def locate(row_ids, block_order, doc_ids):
    block_len = doc_ids.shape[0] // block_order.shape[0]
    block_id = row_ids // block_len
    slot_table = jnp.arange(block_order.shape[0], dtype=jnp.int32)
    starts = jnp.sum(
        jnp.where(block_id[:, None] == slot_table[None, :], block_order[None, :], 0), axis=1
    )
    places = starts * block_len + row_ids % block_len
    return (places, jnp.take(doc_ids, places))


def attend_block(
    running, key_block, value_block, key_place, key_doc, query_heads, query_place, query_doc
):
    visible = (key_place[None, :] <= query_place[:, None]) & (
        key_doc[None, :] == query_doc[:, None]
    )
    row_top, row_total, row_accum = running
    scores = jnp.einsum(
        "thd,dk->thk", query_heads, key_block, preferred_element_type=jnp.float32
    ) * key_block.shape[0] ** (-0.5)
    scores = jnp.where(visible[:, None, :], scores, floor_score)
    new_top = jnp.maximum(row_top, jnp.max(scores, axis=2))
    factor = jnp.exp(row_top - new_top)
    weights = jnp.where(visible[:, None, :], jnp.exp(scores - new_top[:, :, None]), 0.0)
    row_total = row_total * factor + jnp.sum(weights, axis=2)
    mixed = jnp.einsum(
        "thk,dk->thd", weights.astype(jnp.bfloat16), value_block, preferred_element_type=jnp.float32
    )
    row_accum = row_accum * factor[:, :, None] + mixed
    return (new_top, row_total, row_accum)


def attend_span(
    running, key_piece, value_piece, query_heads, query_place, query_doc, block_order, doc_ids
):
    key_count = key_piece.shape[1]
    block_width = 1024
    rounds = key_count // block_width
    places, doc_list = locate(jnp.arange(key_count, dtype=jnp.int32), block_order, doc_ids)

    def one_round(round_index, current):
        offset = round_index * block_width
        return attend_block(
            current,
            lax.dynamic_slice_in_dim(key_piece, offset, block_width, 1),
            lax.dynamic_slice_in_dim(value_piece, offset, block_width, 1),
            lax.dynamic_slice_in_dim(places, offset, block_width, 0),
            lax.dynamic_slice_in_dim(doc_list, offset, block_width, 0),
            query_heads,
            query_place,
            query_doc,
        )

    return lax.fori_loop(0, rounds, one_round, running)


def normalize(running, row_count):
    row_top, row_total, row_accum = running
    return (row_accum / row_total[:, :, None]).astype(jnp.bfloat16).reshape(row_count, -1)


def shards(queries, key_heads, value_heads, out_weight, block_order, doc_ids):
    row_count = queries.shape[0]
    head_count = queries.shape[1] // HD
    group_size = lax.axis_size("head") // KVH
    lane_index = lax.axis_index("head")
    kv_start = lane_index // group_size * HD
    key_part = lax.dynamic_slice_in_dim(key_heads, kv_start, HD, 0)
    value_part = lax.dynamic_slice_in_dim(value_heads, kv_start, HD, 0)
    ctx_index = lax.axis_index("ctx")
    own_rows = ctx_index * row_count + jnp.arange(row_count, dtype=jnp.int32)
    query_place, query_doc = locate(own_rows, block_order, doc_ids)
    query_heads = queries.reshape(row_count, head_count, HD)
    running = attend_span(
        (
            jnp.full((row_count, head_count), floor_score, jnp.float32),
            jnp.zeros((row_count, head_count), jnp.float32),
            jnp.zeros((row_count, head_count, HD), jnp.float32),
        ),
        lax.all_gather(key_part, "ctx", axis=1, tiled=True),
        lax.all_gather(value_part, "ctx", axis=1, tiled=True),
        query_heads,
        query_place,
        query_doc,
        block_order,
        doc_ids,
    )
    context = normalize(running, row_count)
    partial_sum = jnp.dot(context, out_weight, preferred_element_type=jnp.float32)
    return lax.psum_scatter(
        partial_sum.astype(jnp.bfloat16), "head", scatter_dimension=1, tiled=True
    )


def solution(mesh):
    placed = (P("ctx", "head"), P(None, "ctx"), P(None, "ctx"), P("head", None), P(), P())
    return jax.shard_map(
        shards, mesh=mesh, in_specs=placed, out_specs=P("ctx", "head"), check_vma=False
    )
```

profile of v0, /device:TPU:20, one launch (start us, length us, event | category | flops | bytes accessed | tf_op | source)
XLA Modules:
  0.0 468.2 jit_solution(731710215248140285)
XLA Ops:
  6.5 1.6 copy-done
  8.1 0.8 copy.20
  9.0 1.7 constant_dynamic-slice_fusion.1
  10.8 0.0 reduce-scatter.2.cloned.1.call-start
  10.8 0.7 select_reduce_fusion.1
  11.6 0.8 select_reduce_fusion
  12.4 5.8 %gather_fusion.1 = s32[1024]{0:T(1024)S(1)} fusion(s32[4096]{0:T(1024)} %param.13, s32[1024]{0:T(1024)S(1)} %broadcast_clamp_fusion.1), kind=kCustom, calls=%fused_computation.1 | custom fusion | bytes 12288 | tf_op jit(solution)/shard_map/jit(_take)/gather | solution.py:21
  18.3 23.0 %gather_fusion = s32[4096]{0:T(1024)S(1)} fusion(s32[4096]{0:T(1024)S(1)} %copy-done.2, s32[4096]{0:T(1024)S(1)} %broadcast_clamp_fusion), kind=kCustom, calls=%fused_computation | custom fusion | bytes 49152 | tf_op jit(solution)/shard_map/jit(_take)/gather | solution.py:21
  41.3 2.9 copy.16
  44.2 2.4 copy.17
  46.6 18.8 %all-gather.5.cloned.1.call-done = bf16[128,4096]{1,0:T(8,128)(2,1)} async-done(((bf16[128,1024]{1,0:T(8,128)(2,1)}), bf16[128,4096]{1,0:T(8,128)(2,1)}) %all-gather.5.cloned.1.call-update) | async-done | bytes 1048592 | tf_op jit(solution)/shard_map/all_gather | solution.py:94
  65.4 196.0 %while.18 = (s32[]{:T(128)}, f32[1024,8]{0,1:T(8,128)S(1)}, f32[1024,8]{0,1:T(8,128)S(1)}, f32[1024,8,128]{2,0,1:T(8,128)}, s32[4096]{0:T(1024)S(1)}, /*index=5*...) while((s32[]{:T(128)}, f32[1024,8]{0,1:T(8,128)S(1)}, ...), condition=%wide.region_5.6_spmd.clone, body=%wide.region_2.5_spmd.clone.sunk | while | flops 4410351616 | bytes 116424928 | solution.py:67
  65.4 1.2 compare_and_fusion.2
  66.5 14.9 %fusion.51 = (f32[1024,8]{0,1:T(8,128)S(1)}, f32[1024,1024,8]{1,0,2:T(8,128)}) fusion(pred[1024,1024]{0,1:T(8,128)(4,1)S(1)} %compare_and_fusion.2, bf16[1024,8,128]{2,0,1:T(8,128)(2,1)} %get-tuple-element.394, bf16[128,4096]{0,1:T(8,128)(2,1)} %get-tuple-element.393, s32[]{:T(128)S(6)} %select_n.212), kind=kOutput, calls=%fused_computation.4.clone.1 | convolution fusion | flops 2172641280 | bytes 36995076 | tf_op jit(solution)/shard_map/while/body/eval_jaxpr/thd,dk->thk/dot_general | solution.py:31
  81.4 14.7 %fusion.52 = f32[1024,8]{0,1:T(8,128)S(1)} fusion(f32[1024,1024,8]{1,0,2:T(8,128)} %get-tuple-element.352, f32[1024,8]{0,1:T(8,128)S(1)} %select_maximum_fusion.2, pred[1024,1024]{0,1:T(8,128)(4,1)S(1)} %compare_and_fusion.2), kind=kLoop, calls=%fused_computation.6.clone.1 | loop fusion | flops 41934848 | bytes 34668544 | tf_op jit(solution)/shard_map/while/body/eval_jaxpr/reduce_sum | solution.py:38
  96.2 17.4 %fusion.54 = f32[1024,8,128]{2,0,1:T(8,128)} fusion(f32[1024,8,128]{2,0,1:T(8,128)} %get-tuple-element.373, f32[1024,8]{0,1:T(8,128)S(1)} %get-tuple-element.354, pred[]{:T(512)S(6)} %compare.25, f32[1024,1024,8]{1,0,2:T(8,128)} %get-tuple-element.352, f32[1024,8]{0,1:T(8,128)S(1)} %select_maximum_fusion.2, ...), kind=kOutput, calls=%fused_computation.10.clone.1 | convolution fusion | flops 2192572416 | bytes 43319300 | tf_op jit(solution)/shard_map/while/body/eval_jaxpr/thk,dk->thd/dot_general | solution.py:39
  113.7 1.2 compare_and_fusion.2
  114.8 14.9 %fusion.51 = (f32[1024,8]{0,1:T(8,128)S(1)}, f32[1024,1024,8]{1,0,2:T(8,128)}) fusion(pred[1024,1024]{0,1:T(8,128)(4,1)S(1)} %compare_and_fusion.2, bf16[1024,8,128]{2,0,1:T(8,128)(2,1)} %get-tuple-element.394, bf16[128,4096]{0,1:T(8,128)(2,1)} %get-tuple-element.393, s32[]{:T(128)S(6)} %select_n.212), kind=kOutput, calls=%fused_computation.4.clone.1 | convolution fusion | flops 2172641280 | bytes 36995076 | tf_op jit(solution)/shard_map/while/body/eval_jaxpr/thd,dk->thk/dot_general | solution.py:31
  129.7 14.7 %fusion.52 = f32[1024,8]{0,1:T(8,128)S(1)} fusion(f32[1024,1024,8]{1,0,2:T(8,128)} %get-tuple-element.352, f32[1024,8]{0,1:T(8,128)S(1)} %select_maximum_fusion.2, pred[1024,1024]{0,1:T(8,128)(4,1)S(1)} %compare_and_fusion.2), kind=kLoop, calls=%fused_computation.6.clone.1 | loop fusion | flops 41934848 | bytes 34668544 | tf_op jit(solution)/shard_map/while/body/eval_jaxpr/reduce_sum | solution.py:38
  144.5 18.4 %fusion.54 = f32[1024,8,128]{2,0,1:T(8,128)} fusion(f32[1024,8,128]{2,0,1:T(8,128)} %get-tuple-element.373, f32[1024,8]{0,1:T(8,128)S(1)} %get-tuple-element.354, pred[]{:T(512)S(6)} %compare.25, f32[1024,1024,8]{1,0,2:T(8,128)} %get-tuple-element.352, f32[1024,8]{0,1:T(8,128)S(1)} %select_maximum_fusion.2, ...), kind=kOutput, calls=%fused_computation.10.clone.1 | convolution fusion | flops 2192572416 | bytes 43319300 | tf_op jit(solution)/shard_map/while/body/eval_jaxpr/thk,dk->thd/dot_general | solution.py:39
  162.9 1.2 compare_and_fusion.2
  164.1 14.9 %fusion.51 = (f32[1024,8]{0,1:T(8,128)S(1)}, f32[1024,1024,8]{1,0,2:T(8,128)}) fusion(pred[1024,1024]{0,1:T(8,128)(4,1)S(1)} %compare_and_fusion.2, bf16[1024,8,128]{2,0,1:T(8,128)(2,1)} %get-tuple-element.394, bf16[128,4096]{0,1:T(8,128)(2,1)} %get-tuple-element.393, s32[]{:T(128)S(6)} %select_n.212), kind=kOutput, calls=%fused_computation.4.clone.1 | convolution fusion | flops 2172641280 | bytes 36995076 | tf_op jit(solution)/shard_map/while/body/eval_jaxpr/thd,dk->thk/dot_general | solution.py:31
  179.0 14.7 %fusion.52 = f32[1024,8]{0,1:T(8,128)S(1)} fusion(f32[1024,1024,8]{1,0,2:T(8,128)} %get-tuple-element.352, f32[1024,8]{0,1:T(8,128)S(1)} %select_maximum_fusion.2, pred[1024,1024]{0,1:T(8,128)(4,1)S(1)} %compare_and_fusion.2), kind=kLoop, calls=%fused_computation.6.clone.1 | loop fusion | flops 41934848 | bytes 34668544 | tf_op jit(solution)/shard_map/while/body/eval_jaxpr/reduce_sum | solution.py:38
  193.7 18.4 %fusion.54 = f32[1024,8,128]{2,0,1:T(8,128)} fusion(f32[1024,8,128]{2,0,1:T(8,128)} %get-tuple-element.373, f32[1024,8]{0,1:T(8,128)S(1)} %get-tuple-element.354, pred[]{:T(512)S(6)} %compare.25, f32[1024,1024,8]{1,0,2:T(8,128)} %get-tuple-element.352, f32[1024,8]{0,1:T(8,128)S(1)} %select_maximum_fusion.2, ...), kind=kOutput, calls=%fused_computation.10.clone.1 | convolution fusion | flops 2192572416 | bytes 43319300 | tf_op jit(solution)/shard_map/while/body/eval_jaxpr/thk,dk->thd/dot_general | solution.py:39
  212.1 1.2 compare_and_fusion.2
  213.3 14.9 %fusion.51 = (f32[1024,8]{0,1:T(8,128)S(1)}, f32[1024,1024,8]{1,0,2:T(8,128)}) fusion(pred[1024,1024]{0,1:T(8,128)(4,1)S(1)} %compare_and_fusion.2, bf16[1024,8,128]{2,0,1:T(8,128)(2,1)} %get-tuple-element.394, bf16[128,4096]{0,1:T(8,128)(2,1)} %get-tuple-element.393, s32[]{:T(128)S(6)} %select_n.212), kind=kOutput, calls=%fused_computation.4.clone.1 | convolution fusion | flops 2172641280 | bytes 36995076 | tf_op jit(solution)/shard_map/while/body/eval_jaxpr/thd,dk->thk/dot_general | solution.py:31
  228.2 14.7 %fusion.52 = f32[1024,8]{0,1:T(8,128)S(1)} fusion(f32[1024,1024,8]{1,0,2:T(8,128)} %get-tuple-element.352, f32[1024,8]{0,1:T(8,128)S(1)} %select_maximum_fusion.2, pred[1024,1024]{0,1:T(8,128)(4,1)S(1)} %compare_and_fusion.2), kind=kLoop, calls=%fused_computation.6.clone.1 | loop fusion | flops 41934848 | bytes 34668544 | tf_op jit(solution)/shard_map/while/body/eval_jaxpr/reduce_sum | solution.py:38
  242.9 18.4 %fusion.54 = f32[1024,8,128]{2,0,1:T(8,128)} fusion(f32[1024,8,128]{2,0,1:T(8,128)} %get-tuple-element.373, f32[1024,8]{0,1:T(8,128)S(1)} %get-tuple-element.354, pred[]{:T(512)S(6)} %compare.25, f32[1024,1024,8]{1,0,2:T(8,128)} %get-tuple-element.352, f32[1024,8]{0,1:T(8,128)S(1)} %select_maximum_fusion.2, ...), kind=kOutput, calls=%fused_computation.10.clone.1 | convolution fusion | flops 2192572416 | bytes 43319300 | tf_op jit(solution)/shard_map/while/body/eval_jaxpr/thk,dk->thd/dot_general | solution.py:39
  261.3 5.5 %copy.18 = f32[1024,8,128]{0,2,1:T(8,128)} copy(f32[1024,8,128]{2,0,1:T(8,128)} %get-tuple-element.190) | data formatting | bytes 8388608 | tf_op jit(solution)/shard_map/while | solution.py:67
  266.9 2.8 divide_convert_fusion
  269.6 26.2 %convolution_convert_fusion = bf16[1024,8192]{1,0:T(8,128)(2,1)} fusion(bf16[1024,1024]{0,1:T(8,128)(2,1)S(1)} %bitcast.43, bf16[1024,8192]{1,0:T(8,128)(2,1)} %param.11), kind=kOutput, calls=%fused_computation.26 | convolution fusion | flops 17188257792 | bytes 35651584 | tf_op jit(solution)/shard_map/dot_general | solution.py:102
  295.9 165.8 %reduce-scatter.2.cloned.1.call-done = bf16[1024,1024]{1,0:T(8,128)(2,1)} async-done(((bf16[1024,8192]{1,0:T(8,128)(2,1)}), bf16[1024,1024]{1,0:T(8,128)(2,1)}) %reduce-scatter.2.cloned.1.call-update) | async-done | bytes 2097168 | tf_op jit(solution)/shard_map/reduce_scatter | solution.py:103
  (45 shorter events, 0.4 us)
Async XLA Ops:
  6.5 1.6 copy-start
  6.5 11.7 %copy-start.2 = (s32[4096]{0:T(1024)S(1)}, s32[4096]{0:T(1024)}, u32[]{:S(2)}) copy-start(s32[4096]{0:T(1024)} %param.13) | copy-start | bytes 49156
  6.5 40.1 %all-gather.3.cloned.1.call-start = ((), (), s32[]{:S(2)}) async-start(), calls=%async_computation.1 | async-start | bytes 1310720 | tf_op jit(solution)/shard_map/all_gather | solution.py:93
  9.0 56.4 %all-gather.5.cloned.1.call-start = ((), (), s32[]{:S(2)}) async-start(), calls=%async_computation.2 | async-start | bytes 1310720 | tf_op jit(solution)/shard_map/all_gather | solution.py:94
  10.8 450.9 %reduce-scatter.2.cloned.1.call-start = ((), (), s32[]{:S(2)}) async-start(), calls=%async_computation.3 | async-start | bytes 18874368 | tf_op jit(solution)/shard_map/reduce_scatter | solution.py:103
  295.8 165.8 %copy-start.1 = (bf16[1024,1024]{1,0:T(8,128)(2,1)S(1)}, bf16[1024,1024]{1,0:T(8,128)(2,1)}, u32[]{:S(2)}) copy-start(bf16[1024,1024]{1,0:T(8,128)(2,1)} %param.9) | copy-start | bytes 6291460
Sparse Core Ops, SparseCore 0:
  9.2 27.6 all-gather.2
  38.7 26.6 all-gather.4
  296.0 165.6 reduce-scatter.1
where the time goes:
time: 474 us; the launch traced here: 468 us
  waiting for transfers between devices  185 us (39%)
  matrix products  158 us (33%)
  other arithmetic  68.1 us (14%)
  local copies, waits for them, and re-layouts  43.7 us (9%)
  between operations  13.3 us (3%)
    reduce_scatter x1, waiting for transfers between devices, shards(): lax.psum_scatter(partial_sum.astype(jnp.bfloat16), 'head', scatter_dimens...  166 us
    dot_general x4, matrix products, attend_block(): jnp.einsum('thk,dk->thd', weights.astype(jnp.bfloat16), value_block, pref...  72.6 us
    dot_general x4, matrix products, attend_block(): jnp.einsum('thd,dk->thk', query_heads, key_block, preferred_element_type=...  59.5 us
    reduce_sum x4, other arithmetic, attend_block(): row_total = row_total * factor + jnp.sum(weights, axis=2)  58.8 us
    gather x2, local copies, waits for them, and re-layouts, locate(): return (places, jnp.take(doc_ids, places))  28.8 us
    dot_general x1, matrix products, shards(): jnp.dot(context, out_weight, preferred_element_type=jnp.float32)  26.2 us
    all_gather x1, waiting for transfers between devices, shards(): lax.all_gather(value_part, 'ctx', axis=1, tiled=True)  18.8 us
  transfers between devices with their start and end apart: 3, of which 2 were waited for; matrix products, arithmetic and copies ran while one was open for 8% of the time, Pallas kernels for 0%

commit v1 on v0

v1 whole, which is shorter than its diff:
```python
import functools
import math

import jax
import jax.numpy as jnp
from jax import lax
from jax.experimental import pallas as pl
from jax.experimental.pallas import tpu as pltpu
from jax.sharding import PartitionSpec as P

KVH = 8
HD = 128
DOCS = 6
FLOOR = -1e30
TQ = 256
TK = 256
MIB = 1 << 20
SMALL = pl.CostEstimate(flops=1, transcendentals=0, bytes_accessed=1)


def attend_kernel(
    row_tile, block_len, held, heads, n_pieces, scal, q_ref, *rest
):
    pieces, (o_ref, kv, acc, top, sem) = rest[:n_pieces], rest[n_pieces:]
    tile = pl.program_id(0)
    n_own = kv.shape[0]
    n_tiles_all, n_blocks = held
    inv_at = n_tiles_all
    first_at = inv_at + n_blocks
    owner_at = first_at + DOCS

    @pl.when(tile == 0)
    def _():
        copies = []
        for part in range(2):
            of_part = pieces[part * (n_pieces // 2) : (part + 1) * (n_pieces // 2)]
            sources = [piece.at[m] for piece in of_part for m in range(piece.shape[0])]
            for at, source in enumerate(sources):
                target = kv.at[scal[owner_at + at], pl.ds(part * HD, HD), :]
                copies.append(pltpu.make_async_copy(source, target, sem.at[part, at]))
        for copy in copies:
            copy.start()
        kv[:, 2 * HD :, :] = jnp.ones((n_own, HD, kv.shape[2]), kv.dtype)
        for copy in copies:
            copy.wait()

    place = scal[row_tile + tile]
    low = jnp.int32(0)
    rows = place + lax.broadcasted_iota(jnp.int32, (TQ, TK), 0)
    begin = jnp.zeros((TQ, TK), jnp.int32)
    for d in range(DOCS):
        start = scal[first_at + d]
        low = jnp.where(start <= place, start, low)
        begin = jnp.where(rows >= start, start, begin)
    acc[...] = jnp.zeros_like(acc)
    top[...] = jnp.full_like(top, FLOOR)
    scale = math.log2(math.e) / math.sqrt(HD)
    slots = kv.shape[2] // block_len

    def one(step, carry):
        base = step * TK
        slot = scal[inv_at + base // block_len]
        owner = slot // slots
        offset = pl.multiple_of((slot % slots) * block_len + base % block_len, TK)
        keys = kv[owner, 0:HD, pl.ds(offset, TK)]
        values = kv[owner, HD : 3 * HD, pl.ds(offset, TK)]
        cols = base + lax.broadcasted_iota(jnp.int32, (TQ, TK), 1)
        bias = jnp.where((cols <= rows) & (cols >= begin), 0.0, FLOOR)
        for h in range(heads):
            scores = jnp.dot(
                q_ref[:, h * HD : (h + 1) * HD], keys, preferred_element_type=jnp.float32
            )
            scores = scores * scale + bias
            old = top[h]
            new = jnp.maximum(old, jnp.max(scores, axis=1, keepdims=True))
            factor = jnp.exp2(old - new)
            weights = jnp.exp2(scores - jnp.tile(new, (1, TK // HD))).astype(jnp.bfloat16)
            mixed = lax.dot_general(
                weights, values, (((1,), (1,)), ((), ())), preferred_element_type=jnp.float32
            )
            acc[h] = acc[h] * jnp.tile(factor, (1, 2)) + mixed
            top[h] = new
        return carry

    lax.fori_loop(low // TK, (place + TQ - 1) // TK + 1, one, 0)
    for h in range(heads):
        o_ref[:, h * HD : (h + 1) * HD] = (acc[h, :, 0:HD] / acc[h, :, HD:]).astype(o_ref.dtype)


def attend(scal, queries, pieces, row_tile, n_rows, n_blocks, block_len, n_own):
    width = queries.shape[1]
    heads = width // HD
    tiles_all = queries.shape[0] // TQ
    tokens = pieces[0].shape[-1]
    return pl.pallas_call(
        functools.partial(
            attend_kernel, row_tile, block_len, (tiles_all, n_blocks), heads, len(pieces)
        ),
        out_shape=jax.ShapeDtypeStruct((n_rows, width), jnp.bfloat16),
        grid_spec=pltpu.PrefetchScalarGridSpec(
            num_scalar_prefetch=1,
            grid=(n_rows // TQ,),
            in_specs=[pl.BlockSpec((TQ, width), lambda i, s: (row_tile + i, 0))]
            + [pl.BlockSpec(memory_space=pltpu.HBM)] * len(pieces),
            out_specs=pl.BlockSpec((TQ, width), lambda i, s: (i, 0)),
            scratch_shapes=[
                pltpu.VMEM((n_own, 3 * HD, tokens), jnp.bfloat16),
                pltpu.VMEM((heads, TQ, 2 * HD), jnp.float32),
                pltpu.VMEM((heads, TQ, HD), jnp.float32),
                pltpu.SemaphoreType.DMA((2, n_own)),
            ],
        ),
        compiler_params=pltpu.CompilerParams(vmem_limit_bytes=40 * MIB),
        cost_estimate=SMALL,
        name="attend",
    )(scal, queries, *pieces)


def gather_kernel(base_ref, *rest):
    total = base_ref[...]
    for add in rest[:2]:
        total += add[...].astype(jnp.float32)
    rest[-1][...] = total.astype(rest[-1].dtype)


def gather_up(base, adds, into, total_rows, at):
    rows, width = base.shape
    tile = rows // 2
    specs = [pl.BlockSpec((tile, width), lambda i: (i, 0))] * 3
    operands = [base, *adds]
    aliases = {}
    if into is not None:
        specs.append(pl.BlockSpec(memory_space=pl.ANY))
        operands.append(into)
        aliases = {3: 0}
    return pl.pallas_call(
        gather_kernel,
        out_shape=jax.ShapeDtypeStruct((total_rows, width), jnp.bfloat16),
        grid=(2,),
        in_specs=specs,
        out_specs=pl.BlockSpec((tile, width), lambda i: (2 * at + i, 0)),
        input_output_aliases=aliases,
        cost_estimate=SMALL,
        name="gather_up",
    )(*operands)


def unit_kernel(n_add, n_out, scal, own_ref, other_ref, w_ref, wp_ref, *rest):
    adds, outs = rest[:n_add], rest[n_add:]

    def product(out):
        total = jnp.dot(own_ref[...], w_ref[...], preferred_element_type=jnp.float32)
        total += jnp.dot(other_ref[...], wp_ref[...], preferred_element_type=jnp.float32)
        for add in adds:
            total += add[...].astype(jnp.float32)
        out[...] = total.astype(out.dtype)

    for n, out in enumerate(outs):

        @pl.when((scal[1] == 1) & ((n_out == 1) | (pl.program_id(0) == n)))
        def _():
            product(out)


def in_hbm(value):
    return pltpu.with_memory_space_constraint(value, pltpu.HBM)


def unit(scal, own, other, weight, weight_p, adds, columns, tn, n_out, out_type):
    rows, depth = own.shape
    per = columns // tn

    def column(j, s):
        return j + s[2] * (1 - 2 * j) if n_out > 1 else j

    specs = [
        pl.BlockSpec((rows, depth), lambda j, s: (0, 0)),
        pl.BlockSpec((rows, depth), lambda j, s: (0, 0)),
        pl.BlockSpec((depth, tn), lambda j, s: (0, (s[0] + column(j, s)) * s[1])),
        pl.BlockSpec((depth, tn), lambda j, s: (0, (s[0] + column(j, s)) * s[1])),
    ] + [pl.BlockSpec((rows, tn), lambda j, s: (0, column(j, s) * s[1]))] * len(adds)
    out_spec = pl.BlockSpec((rows, tn), lambda j, s: (0, j if n_out == 1 else 0))
    out_shape = jax.ShapeDtypeStruct((rows, columns if n_out == 1 else tn), out_type)
    return pl.pallas_call(
        functools.partial(unit_kernel, len(adds), n_out),
        out_shape=[out_shape] * n_out,
        grid_spec=pltpu.PrefetchScalarGridSpec(
            num_scalar_prefetch=1,
            grid=(per,),
            in_specs=specs,
            out_specs=[out_spec] * n_out,
        ),
        compiler_params=pltpu.CompilerParams(vmem_limit_bytes=40 * MIB),
        cost_estimate=SMALL,
        name="unit",
    )(scal, own, other, weight, weight_p, *adds)


def own_kernel(n, scal, *refs):
    mine, other = refs[:n], refs[n : 2 * n]
    w_ref, wp_ref = refs[2 * n : 2 * n + 2]
    for a, b, out in zip(mine, other, refs[2 * n + 2 :]):
        total = jnp.dot(a[...], w_ref[...], preferred_element_type=jnp.float32)
        out[...] = total + jnp.dot(b[...], wp_ref[...], preferred_element_type=jnp.float32)


def own_product(scal, mine, other, weight, weight_p, columns):
    rows, depth = mine[0].shape
    n, tn = len(mine), 256
    per = columns // tn
    row_spec = pl.BlockSpec((rows, depth), lambda j, s: (0, 0))
    w_spec = pl.BlockSpec((depth, tn), lambda j, s: (0, s[0] * per + j))
    return pl.pallas_call(
        functools.partial(own_kernel, n),
        out_shape=[jax.ShapeDtypeStruct((rows, columns), jnp.float32)] * n,
        grid_spec=pltpu.PrefetchScalarGridSpec(
            num_scalar_prefetch=1,
            grid=(per,),
            in_specs=[row_spec] * (2 * n) + [w_spec] * 2,
            out_specs=[pl.BlockSpec((rows, tn), lambda j, s: (0, j))] * n,
        ),
        compiler_params=pltpu.CompilerParams(vmem_limit_bytes=40 * MIB),
        cost_estimate=SMALL,
        name="own_product",
    )(scal, *mine, *other, weight, weight_p)


def tables(block_order, doc_ids, row_count, owners):
    n_blocks = block_order.shape[0]
    block_len = doc_ids.shape[0] // n_blocks
    ids = jnp.arange(n_blocks, dtype=jnp.int32)
    inverse = jnp.sum(jnp.where(block_order[None, :] == ids[:, None], ids[None, :], 0), axis=1)
    first = jnp.sum(
        (doc_ids[None, :] < jnp.arange(DOCS, dtype=jnp.int32)[:, None]).astype(jnp.int32), axis=1
    )
    row = lax.axis_index("ctx") * row_count + TQ * jnp.arange(row_count // TQ, dtype=jnp.int32)
    slot = row // block_len
    start = jnp.sum(jnp.where(slot[:, None] == ids[None, :], block_order[None, :], 0), axis=1)
    places = start * block_len + row % block_len
    return jnp.concatenate([places, inverse, first, owners]).astype(jnp.int32)


def own_head(of_heads):
    group = lax.axis_size("head") // KVH
    return lax.dynamic_slice_in_dim(of_heads, lax.axis_index("head") // group * HD, HD, 0)


def general(queries, key_heads, value_heads, out_weight, block_order, doc_ids):
    row_count = queries.shape[0]
    n_own = lax.axis_size("ctx")
    n_blocks = block_order.shape[0]
    block_len = doc_ids.shape[0] // n_blocks
    gathered = [lax.all_gather(own_head(a), "ctx", axis=0) for a in (key_heads, value_heads)]
    scal = tables(block_order, doc_ids, row_count, jnp.arange(n_own, dtype=jnp.int32))
    context = attend(scal, queries, gathered, 0, row_count, n_blocks, block_len, n_own)
    partial_sum = jnp.dot(context, out_weight, preferred_element_type=jnp.float32)
    return lax.psum_scatter(
        partial_sum.astype(jnp.bfloat16), "head", scatter_dimension=1, tiled=True
    )


CHUNK = 256


def tied(value, *others):
    if not others:
        return value
    return lax.optimization_barrier((value, *others))[0]


def named(step, name):
    def run(*args):
        with jax.named_scope(name + "".join(str(a) for a in args if isinstance(a, int))):
            return step(*args)

    return run


def line(queries, key_heads, value_heads, out_weight, block_order, doc_ids):
    row_count, depth = queries.shape
    n_blocks = block_order.shape[0]
    block_len = doc_ids.shape[0] // n_blocks
    ctx, head = lax.axis_index("ctx"), lax.axis_index("head")
    chip, core = head // 2, head % 2
    far = jnp.where(core == 0, chip, 3 - chip)
    swap = [(h, h ^ 1) for h in range(8)]
    along = [[(c, c ^ k) for c in range(4)] for k in (1, 2)]

    keys, values = own_head(key_heads), own_head(value_heads)
    keys_1 = lax.ppermute(keys, "ctx", along[0])
    values_2 = lax.ppermute(values, "ctx", along[1])
    values_1 = lax.ppermute(values, "ctx", along[0])
    keys_2 = lax.ppermute(keys, "ctx", along[1])
    keys_3 = lax.ppermute(keys_1, "ctx", along[1])
    values_3 = lax.ppermute(values_2, "ctx", along[0])
    weight_p = lax.ppermute(out_weight, "head", swap)
    owners = jnp.stack([ctx, ctx ^ 1, ctx ^ 2, ctx ^ 3]).astype(jnp.int32)
    scal = tables(block_order, doc_ids, row_count, owners)
    pieces = [keys, keys_1, keys_2, keys_3, values, values_1, values_2, values_3]
    pieces = [in_hbm(p[None]) for p in pieces]
    queries = in_hbm(queries)

    chunks = row_count // CHUNK
    mine, other, base, received = {}, {}, {}, {}
    def attention(k, *behind):
        mine[k] = attend(
            tied(scal, *behind), queries, pieces, k * CHUNK // TQ, CHUNK, n_blocks, block_len, 4
        )
        other[k] = lax.ppermute(mine[k], "head", swap)

    def tick(k, s, *behind):
        valid = (far <= s) & (far <= 2)
        mirrored = 3 - s + far
        dest = jnp.where(core == 0, mirrored, 3 - mirrored)
        job = jnp.stack([jnp.where(valid, 2 * dest, 0), valid, core]).astype(jnp.int32)
        job = tied(job, *behind)
        adds = [] if s == 0 else [received[k, s - 1][0]]
        last = s == 2
        sent[k, s] = unit(
            job, mine[k], other[k], out_weight, weight_p, adds, 2 * depth, depth,
            2 if last else 1, jnp.bfloat16,
        )
        received[k, s] = []
        for cross in range(2 if last else 1):
            pairs = []
            for f in range(min(s, 2) + 1):
                pairs.append((2 * f, 2 * (f + 1) + cross))
                pairs.append((2 * (3 - f) + 1, 2 * (2 - f) + 1 - cross))
            received[k, s].append(in_hbm(lax.ppermute(sent[k, s][cross], "head", pairs)))

    own_job = jnp.stack([head, 1, 0]).astype(jnp.int32)

    def own_part(*behind):
        parts = own_product(
            tied(own_job, *behind), [in_hbm(mine[k]) for k in range(chunks)],
            [in_hbm(other[k]) for k in range(chunks)], out_weight, weight_p, depth,
        )
        base.update(enumerate(parts))

    def finish(k):
        result[0] = gather_up(base[k], received[k, 2], result[0], row_count, k)

    sent = {}
    result = [None]
    attention, tick, own_part, finish = [
        named(f, n) for f, n in ((attention, "a"), (tick, "t"), (own_part, "o"), (finish, "f"))
    ]
    attention(0)
    attention(1, mine[0])
    tick(0, 0)
    attention(2, mine[1], sent[0, 0][0])
    tick(1, 0)
    attention(3, mine[2], received[0, 0][0])
    tick(2, 0, received[0, 0][0])
    tick(3, 0, received[1, 0][0])
    for s in (1, 2):
        if s == 2:
            own_part()
        for k in range(chunks):
            tick(k, s, *([base[0]] if (k, s) == (0, 2) else []))
    for k in range(chunks):
        finish(k)
    return result[0]


def shards(*args):
    square = lax.axis_size("ctx") == 4 and lax.axis_size("head") == 8
    return (line if square else general)(*args)


def solution(mesh):
    placed = (P("ctx", "head"), P(None, "ctx"), P(None, "ctx"), P("head", None), P(), P())
    return jax.shard_map(
        shards, mesh=mesh, in_specs=placed, out_specs=P("ctx", "head"), check_vma=False
    )
```

time: 474 us -> 192 us (0.41)
  waiting for transfers between devices: 185 us -> 19.3 us
  matrix products: 158 us -> 0 us
  Pallas kernels: 0 us -> 94.2 us
  other arithmetic: 68.1 us -> 2.8 us
  starting transfers between devices: 0.09 us -> 61.6 us
  local copies, waits for them, and re-layouts: 43.7 us -> 11.6 us
  between operations: 13.3 us -> 0.68 us
    reduce_scatter x1 -> x0, waiting for transfers between devices: 166 us -> none  [shards(): lax.psum_scatter(partial_sum.astype(jnp.bfloat16), 'head', scatter_dimens...]
    dot_general x9 -> x0, matrix products: 158 us -> none  [the longest x4 72.6 us: attend_block(): jnp.einsum('thk,dk->thd', weights.astype(jnp.bfloat16), value_block, pref...]
    pallas_call x0 -> x21, Pallas kernels: none -> 94.2 us  [the longest x12 50.4 us: unit(): pl.pallas_call(functools.partial(unit_kernel, len(adds), n_out), out_shap...]
    ppermute x0 -> x27, starting transfers between devices: none -> 61.6 us  [the longest x16 49.5 us: tick(): lax.ppermute(sent[k, s][cross], 'head', pairs)]
    reduce_sum x6 -> x3, other arithmetic: 60.3 us -> 2.47 us  [the longest x1 0.87 us: tables(): jnp.sum((doc_ids[None, :] < jnp.arange(DOCS, dtype=jnp.int32)[:, None]).a...]
    gather x2 -> x0, local copies, waits for them, and re-layouts: 28.8 us -> none  [locate(): return (places, jnp.take(doc_ids, places))]
    ppermute x0 -> x27, waiting for transfers between devices: none -> 19.3 us  [the longest x16 7.83 us: tick(): lax.ppermute(sent[k, s][cross], 'head', pairs)]
    all_gather x2 -> x0, waiting for transfers between devices: 18.8 us -> none  [the longest x1 18.8 us: shards(): lax.all_gather(value_part, 'ctx', axis=1, tiled=True)]
  transfers between devices with their start and end apart: 3 -> 27, of which waited for: 2 -> 5; matrix products, arithmetic and copies ran while one was open for 8% -> 4% of each run, Pallas kernels for 0% -> 48%
where the time goes in v1:
time: 192 us; the launch traced here: 190 us
  Pallas kernels  94.2 us (49%)
  starting transfers between devices  61.6 us (32%)
  waiting for transfers between devices  19.3 us (10%)
  local copies, waits for them, and re-layouts  11.6 us (6%)
  other arithmetic  2.8 us (1%)
    pallas_call x12, Pallas kernels, unit(): pl.pallas_call(functools.partial(unit_kernel, len(adds), n_out), out_shap...  50.4 us
    ppermute x16, starting transfers between devices, tick(): lax.ppermute(sent[k, s][cross], 'head', pairs)  49.5 us
    pallas_call x4, Pallas kernels, attend(): pl.pallas_call(functools.partial(attend_kernel, row_tile, block_len, (til...  26 us
    pallas_call x4, Pallas kernels, gather_up(): pl.pallas_call(gather_kernel, out_shape=jax.ShapeDtypeStruct((total_rows,...  9.33 us
    pallas_call x1, Pallas kernels, own_product(): pl.pallas_call(functools.partial(own_kernel, n), out_shape=[jax.ShapeDtyp...  8.56 us
    ppermute x16, waiting for transfers between devices, tick(): lax.ppermute(sent[k, s][cross], 'head', pairs)  7.83 us
    ppermute x4, starting transfers between devices, attention(): other[k] = lax.ppermute(mine[k], 'head', swap)  7.01 us
    unnamed x72, local copies, waits for them, and re-layouts  6.63 us
  transfers between devices with their start and end apart: 27, of which 5 were waited for; matrix products, arithmetic and copies ran while one was open for 4% of the time, Pallas kernels for 48%

profile of v1, /device:TPU:20, one launch (start us, length us, event | category | flops | bytes accessed | tf_op | source)
XLA Modules:
  0.0 190.2 jit_solution(15825496551531536)
XLA Ops:
  8.4 4.4 %collective-permute-done.4 = bf16[128,1024]{1,0:T(8,128)(2,1)S(1)} collective-permute-done((bf16[128,1024]{1,0:T(8,128)(2,1)}, bf16[128,1024]{1,0:T(8,128)(2,1)S(1)}, u32[]{:S(2)}, u32[]{:S(2)}) %collective-permute-start.4) | collective-permute-done | bytes 262176 | tf_op jit(solution)/shard_map/ppermute | solution.py:291
  13.2 3.5 %collective-permute-done = bf16[128,1024]{1,0:T(8,128)(2,1)S(1)} collective-permute-done((bf16[128,1024]{1,0:T(8,128)(2,1)}, bf16[128,1024]{1,0:T(8,128)(2,1)S(1)}, u32[]{:S(2)}, u32[]{:S(2)}) %collective-permute-start) | collective-permute-done | bytes 262176 | tf_op jit(solution)/shard_map/ppermute | solution.py:290
  21.9 2.2 %collective-permute-done.2 = bf16[128,1024]{1,0:T(8,128)(2,1)} collective-permute-done((bf16[128,1024]{1,0:T(8,128)(2,1)S(1)}, bf16[128,1024]{1,0:T(8,128)(2,1)}, u32[]{:S(2)}, u32[]{:S(2)}) %collective-permute-start.2) | collective-permute-done | bytes 262176 | tf_op jit(solution)/shard_map/ppermute | solution.py:294
  24.1 5.5 %attend.4.own_ref.refs_0_ = bf16[256,1024]{1,0:T(8,128)(2,1)S(1)} custom-call(s32[22]{0:T(128)S(1)} %concatenate.3.scal, bf16[1024,1024]{1,0:T(8,128)(2,1)} %q_ref.7, bf16[1,128,1024]{2,1,0:T(8,128)(2,1)} %fusion.2.rest_0_, bf16[1,128,1024]{2,1,0:T(8,128)(2,1)} %bitcast.30, bf16[1,128,1024]{2,1,0:T(8,128)(2,1)} %bitcast.34, ...), custom_call_target="tpu_custom_call" | custom-call | flops 1 | bytes 1 | tf_op jit(solution)/shard_map/a0/attend/pallas_call | solution.py:95
  29.9 6.5 %attend.5.refs_1_.own_ref = bf16[256,1024]{1,0:T(8,128)(2,1)S(1)} custom-call(s32[22]{0:T(128)S(1)} %concatenate.3.scal, bf16[1024,1024]{1,0:T(8,128)(2,1)} %q_ref.7, bf16[1,128,1024]{2,1,0:T(8,128)(2,1)} %fusion.2.rest_0_, bf16[1,128,1024]{2,1,0:T(8,128)(2,1)} %bitcast.31, bf16[1,128,1024]{2,1,0:T(8,128)(2,1)} %bitcast.35, ...), custom_call_target="tpu_custom_call" | custom-call | flops 1 | bytes 1 | tf_op jit(solution)/shard_map/a1/attend/pallas_call | solution.py:95
  36.9 2.9 %unit.12 = bf16[256,2048]{1,0:T(8,128)(2,1)S(1)} custom-call(s32[3]{0:T(128)S(1)} %add_add_fusion.scal, bf16[256,1024]{1,0:T(8,128)(2,1)S(1)} %attend.4.own_ref.refs_0_, bf16[256,1024]{1,0:T(8,128)(2,1)S(1)} %collective-permute-done.6.other_ref.refs_4_, bf16[1024,8192]{1,0:T(8,128)(2,1)} %w_ref.23, bf16[1024,8192]{1,0:T(8,128)(2,1)} %collective-permute-done.7.wp_ref.refs_9_), custom_call_target="tpu_custom_call" | custom-call | flops 1 | bytes 1 | tf_op jit(solution)/shard_map/t00/unit/pallas_call | solution.py:184
  40.6 2.9 %unit.13 = bf16[256,2048]{1,0:T(8,128)(2,1)S(1)} custom-call(s32[3]{0:T(128)S(1)} %add_add_fusion.scal, bf16[256,1024]{1,0:T(8,128)(2,1)S(1)} %attend.5.refs_1_.own_ref, bf16[256,1024]{1,0:T(8,128)(2,1)S(1)} %collective-permute-done.9.refs_5_.other_ref, bf16[1024,8192]{1,0:T(8,128)(2,1)} %w_ref.23, bf16[1024,8192]{1,0:T(8,128)(2,1)} %collective-permute-done.7.wp_ref.refs_9_), custom_call_target="tpu_custom_call" | custom-call | flops 1 | bytes 1 | tf_op jit(solution)/shard_map/t10/unit/pallas_call | solution.py:184
  44.3 6.5 %attend.6.refs_2_.own_ref = bf16[256,1024]{1,0:T(8,128)(2,1)S(1)} custom-call(s32[22]{0:T(128)S(1)} %concatenate.3.scal, bf16[1024,1024]{1,0:T(8,128)(2,1)} %q_ref.7, bf16[1,128,1024]{2,1,0:T(8,128)(2,1)} %fusion.2.rest_0_, bf16[1,128,1024]{2,1,0:T(8,128)(2,1)} %bitcast.32, bf16[1,128,1024]{2,1,0:T(8,128)(2,1)} %bitcast.36, ...), custom_call_target="tpu_custom_call" | custom-call | flops 1 | bytes 1 | tf_op jit(solution)/shard_map/a2/attend/pallas_call | solution.py:95
  52.0 7.5 %attend.7.refs_3_.own_ref = bf16[256,1024]{1,0:T(8,128)(2,1)S(1)} custom-call(s32[22]{0:T(128)S(1)} %concatenate.3.scal, bf16[1024,1024]{1,0:T(8,128)(2,1)} %q_ref.7, bf16[1,128,1024]{2,1,0:T(8,128)(2,1)} %fusion.2.rest_0_, bf16[1,128,1024]{2,1,0:T(8,128)(2,1)} %bitcast.33, bf16[1,128,1024]{2,1,0:T(8,128)(2,1)} %bitcast.37, ...), custom_call_target="tpu_custom_call" | custom-call | flops 1 | bytes 1 | tf_op jit(solution)/shard_map/a3/attend/pallas_call | solution.py:95
  59.5 5.2 %collective-permute-start.11 = (bf16[256,1024]{1,0:T(8,128)(2,1)S(1)}, bf16[256,1024]{1,0:T(8,128)(2,1)S(1)}, u32[]{:S(2)}, u32[]{:S(2)}) collective-permute-start(bf16[256,1024]{1,0:T(8,128)(2,1)S(1)} %attend.7.refs_3_.own_ref), channel_id=1, source_target_pairs={{0,1},{1,0},{2,3},{3,2},{4,5},{5,4},{6,7},{7,6},{8,9},{9,8},{10,11... | collective-permute-start | bytes 1572872 | tf_op jit(solution)/shard_map/a3/ppermute | solution.py:309
  64.7 3.8 %unit.17 = bf16[256,2048]{1,0:T(8,128)(2,1)} custom-call(s32[3]{0:T(128)S(1)} %add_add_fusion.scal, bf16[256,1024]{1,0:T(8,128)(2,1)S(1)} %attend.6.refs_2_.own_ref, bf16[256,1024]{1,0:T(8,128)(2,1)S(1)} %collective-permute-done.10.refs_6_.other_ref, bf16[1024,8192]{1,0:T(8,128)(2,1)} %w_ref.23, bf16[1024,8192]{1,0:T(8,128)(2,1)} %collective-permute-done.7.wp_ref.refs_9_), custom_call_target="tpu_custom_call" | custom-call | flops 1 | bytes 1 | tf_op jit(solution)/shard_map/t20/unit/pallas_call | solution.py:184
  70.1 3.8 %unit.14 = bf16[256,2048]{1,0:T(8,128)(2,1)} custom-call(s32[3]{0:T(128)S(1)} %add_add_fusion.scal, bf16[256,1024]{1,0:T(8,128)(2,1)S(1)} %attend.7.refs_3_.own_ref, bf16[256,1024]{1,0:T(8,128)(2,1)S(1)} %collective-permute-done.11.refs_7_.other_ref, bf16[1024,8192]{1,0:T(8,128)(2,1)} %w_ref.23, bf16[1024,8192]{1,0:T(8,128)(2,1)} %collective-permute-done.7.wp_ref.refs_9_), custom_call_target="tpu_custom_call" | custom-call | flops 1 | bytes 1 | tf_op jit(solution)/shard_map/t30/unit/pallas_call | solution.py:184
  76.6 3.9 %unit.20 = bf16[256,2048]{1,0:T(8,128)(2,1)} custom-call(s32[3]{0:T(128)S(1)} %add_add_fusion.2.scal, bf16[256,1024]{1,0:T(8,128)(2,1)S(1)} %attend.5.refs_1_.own_ref, bf16[256,1024]{1,0:T(8,128)(2,1)S(1)} %copy-done.18, bf16[1024,8192]{1,0:T(8,128)(2,1)} %w_ref.23, bf16[1024,8192]{1,0:T(8,128)(2,1)} %collective-permute-done.7.wp_ref.refs_9_, ...), custom_call_target="tpu_custom_call" | custom-call | flops 1 | bytes 1 | tf_op jit(solution)/shard_map/t11/unit/pallas_call | solution.py:184
  81.8 3.9 %unit.22 = bf16[256,2048]{1,0:T(8,128)(2,1)} custom-call(s32[3]{0:T(128)S(1)} %add_add_fusion.2.scal, bf16[256,1024]{1,0:T(8,128)(2,1)S(1)} %attend.4.own_ref.refs_0_, bf16[256,1024]{1,0:T(8,128)(2,1)S(1)} %collective-permute-done.6.other_ref.refs_4_, bf16[1024,8192]{1,0:T(8,128)(2,1)} %w_ref.23, bf16[1024,8192]{1,0:T(8,128)(2,1)} %collective-permute-done.7.wp_ref.refs_9_, ...), custom_call_target="tpu_custom_call" | custom-call | flops 1 | bytes 1 | tf_op jit(solution)/shard_map/t01/unit/pallas_call | solution.py:184
  87.2 3.9 %unit.18 = bf16[256,2048]{1,0:T(8,128)(2,1)} custom-call(s32[3]{0:T(128)S(1)} %add_add_fusion.2.scal, bf16[256,1024]{1,0:T(8,128)(2,1)S(1)} %attend.6.refs_2_.own_ref, bf16[256,1024]{1,0:T(8,128)(2,1)S(1)} %collective-permute-done.10.refs_6_.other_ref, bf16[1024,8192]{1,0:T(8,128)(2,1)} %w_ref.23, bf16[1024,8192]{1,0:T(8,128)(2,1)} %collective-permute-done.7.wp_ref.refs_9_, ...), custom_call_target="tpu_custom_call" | custom-call | flops 1 | bytes 1 | tf_op jit(solution)/shard_map/t21/unit/pallas_call | solution.py:184
  92.3 3.0 %unit.15 = bf16[256,2048]{1,0:T(8,128)(2,1)S(1)} custom-call(s32[3]{0:T(128)S(1)} %add_add_fusion.2.scal, bf16[256,1024]{1,0:T(8,128)(2,1)S(1)} %attend.7.refs_3_.own_ref, bf16[256,1024]{1,0:T(8,128)(2,1)S(1)} %copy-done.15, bf16[1024,8192]{1,0:T(8,128)(2,1)} %w_ref.23, bf16[1024,8192]{1,0:T(8,128)(2,1)} %collective-permute-done.7.wp_ref.refs_9_, ...), custom_call_target="tpu_custom_call" | custom-call | flops 1 | bytes 1 | tf_op jit(solution)/shard_map/t31/unit/pallas_call | solution.py:184
  96.9 8.6 %own_product.1 = (f32[256,1024]{1,0:T(8,128)S(1)}, f32[256,1024]{1,0:T(8,128)S(1)}, f32[256,1024]{1,0:T(8,128)S(1)}, f32[256,1024]{1,0:T(8,128)S(1)}) custom-call(s32[3]{0:T(128)S(1)} %pad_add_fusion.scal, bf16[256,1024]{1,0:T(8,128)(2,1)} %copy-done.2, bf16[256,1024]{1,0:T(8,128)(2,1)} %copy-done.8, bf16[256,1024]{1,0:T(8,128)(2,1)} %copy-done.6, ...), custom_call_target="tpu_custom_call" | custom-call | flops 1 | bytes 1 | tf_op jit(solution)/shard_map/o/own_product/pallas_call | solution.py:213
  108.4 5.7 %unit.21 = (bf16[256,1024]{1,0:T(8,128)(2,1)S(1)}, bf16[256,1024]{1,0:T(8,128)(2,1)S(1)}) custom-call(s32[3]{0:T(128)S(1)} %add_add_fusion.1.scal, bf16[256,1024]{1,0:T(8,128)(2,1)S(1)} %copy-done.9, bf16[256,1024]{1,0:T(8,128)(2,1)S(1)} %copy-done.19, bf16[1024,8192]{1,0:T(8,128)(2,1)} %w_ref.23, bf16[1024,8192]{1,0:T(8,128)(2,1)} %collective-permute-done.7.wp_ref.refs_9_, ...), custom_call_target="tpu_custom_call" | custom-call | flops 1 | bytes 1 | tf_op jit(solution)/shard_map/t12/unit/pallas_call | solution.py:184
  114.1 2.1 %collective-permute-start.22 = (bf16[256,1024]{1,0:T(8,128)(2,1)S(1)}, bf16[256,1024]{1,0:T(8,128)(2,1)S(1)}, u32[]{:S(2)}, u32[]{:S(2)}) collective-permute-start(bf16[256,1024]{1,0:T(8,128)(2,1)S(1)} %get-tuple-element.35), channel_id=1, source_target_pairs={{0,2},{7,5},{2,4},{5,3},{4,6},{3,1},{8,10},{15,13},{10,12},{13,11}... | collective-permute-start | bytes 1572872 | tf_op jit(solution)/shard_map/t12/ppermute | solution.py:329
  116.2 5.6 %unit.23 = (bf16[256,1024]{1,0:T(8,128)(2,1)S(1)}, bf16[256,1024]{1,0:T(8,128)(2,1)S(1)}) custom-call(s32[3]{0:T(128)S(1)} %add_add_fusion.1.scal, bf16[256,1024]{1,0:T(8,128)(2,1)S(1)} %copy-done.3, bf16[256,1024]{1,0:T(8,128)(2,1)S(1)} %copy-done.11, bf16[1024,8192]{1,0:T(8,128)(2,1)} %w_ref.23, bf16[1024,8192]{1,0:T(8,128)(2,1)} %collective-permute-done.7.wp_ref.refs_9_, ...), custom_call_target="tpu_custom_call" | custom-call | flops 1 | bytes 1 | tf_op jit(solution)/shard_map/t02/unit/pallas_call | solution.py:184
  123.7 21.4 %collective-permute-start.26 = (bf16[256,1024]{1,0:T(8,128)(2,1)S(1)}, bf16[256,1024]{1,0:T(8,128)(2,1)S(1)}, u32[]{:S(2)}, u32[]{:S(2)}) collective-permute-start(bf16[256,1024]{1,0:T(8,128)(2,1)S(1)} %get-tuple-element.40), channel_id=1, source_target_pairs={{0,3},{7,4},{2,5},{5,2},{4,7},{3,0},{8,11},{15,12},{10,13},{13,10}... | collective-permute-start | bytes 1572872 | tf_op jit(solution)/shard_map/t02/ppermute | solution.py:329
  146.1 2.0 %collective-permute-start.23 = (bf16[256,1024]{1,0:T(8,128)(2,1)S(1)}, bf16[256,1024]{1,0:T(8,128)(2,1)}, u32[]{:S(2)}, u32[]{:S(2)}) collective-permute-start(bf16[256,1024]{1,0:T(8,128)(2,1)S(1)} %get-tuple-element.36), channel_id=1, source_target_pairs={{0,3},{7,4},{2,5},{5,2},{4,7},{3,0},{8,11},{15,12},{10,13},{13,10}... | collective-permute-start | bytes 1572872 | tf_op jit(solution)/shard_map/t12/ppermute | solution.py:329
  148.1 5.6 %unit.19 = (bf16[256,1024]{1,0:T(8,128)(2,1)S(1)}, bf16[256,1024]{1,0:T(8,128)(2,1)S(1)}) custom-call(s32[3]{0:T(128)S(1)} %add_add_fusion.1.scal, bf16[256,1024]{1,0:T(8,128)(2,1)S(1)} %copy-done.7, bf16[256,1024]{1,0:T(8,128)(2,1)S(1)} %copy-done.13, bf16[1024,8192]{1,0:T(8,128)(2,1)} %w_ref.23, bf16[1024,8192]{1,0:T(8,128)(2,1)} %collective-permute-done.7.wp_ref.refs_9_, ...), custom_call_target="tpu_custom_call" | custom-call | flops 1 | bytes 1 | tf_op jit(solution)/shard_map/t22/unit/pallas_call | solution.py:184
  153.7 2.1 %collective-permute-start.19 = (bf16[256,1024]{1,0:T(8,128)(2,1)S(1)}, bf16[256,1024]{1,0:T(8,128)(2,1)S(1)}, u32[]{:S(2)}, u32[]{:S(2)}) collective-permute-start(bf16[256,1024]{1,0:T(8,128)(2,1)S(1)} %get-tuple-element.32), channel_id=1, source_target_pairs={{0,2},{7,5},{2,4},{5,3},{4,6},{3,1},{8,10},{15,13},{10,12},{13,11}... | collective-permute-start | bytes 1572872 | tf_op jit(solution)/shard_map/t22/ppermute | solution.py:329
  155.9 5.6 %unit.16 = (bf16[256,1024]{1,0:T(8,128)(2,1)S(1)}, bf16[256,1024]{1,0:T(8,128)(2,1)S(1)}) custom-call(s32[3]{0:T(128)S(1)} %add_add_fusion.1.scal, bf16[256,1024]{1,0:T(8,128)(2,1)S(1)} %copy-done.5, bf16[256,1024]{1,0:T(8,128)(2,1)S(1)} %copy-done.16, bf16[1024,8192]{1,0:T(8,128)(2,1)} %w_ref.23, bf16[1024,8192]{1,0:T(8,128)(2,1)} %collective-permute-done.7.wp_ref.refs_9_, ...), custom_call_target="tpu_custom_call" | custom-call | flops 1 | bytes 1 | tf_op jit(solution)/shard_map/t32/unit/pallas_call | solution.py:184
  161.5 3.0 %collective-permute-start.20 = (bf16[256,1024]{1,0:T(8,128)(2,1)S(1)}, bf16[256,1024]{1,0:T(8,128)(2,1)}, u32[]{:S(2)}, u32[]{:S(2)}) collective-permute-start(bf16[256,1024]{1,0:T(8,128)(2,1)S(1)} %get-tuple-element.33), channel_id=1, source_target_pairs={{0,3},{7,4},{2,5},{5,2},{4,7},{3,0},{8,11},{15,12},{10,13},{13,10}... | collective-permute-start | bytes 1572872 | tf_op jit(solution)/shard_map/t22/ppermute | solution.py:329
  167.3 5.0 %collective-permute-start.16 = (bf16[256,1024]{1,0:T(8,128)(2,1)S(1)}, bf16[256,1024]{1,0:T(8,128)(2,1)}, u32[]{:S(2)}, u32[]{:S(2)}) collective-permute-start(bf16[256,1024]{1,0:T(8,128)(2,1)S(1)} %get-tuple-element.29), channel_id=1, source_target_pairs={{0,3},{7,4},{2,5},{5,2},{4,7},{3,0},{8,11},{15,12},{10,13},{13,10}... | collective-permute-start | bytes 1572872 | tf_op jit(solution)/shard_map/t32/ppermute | solution.py:329
  172.3 2.3 %gather_up.4.rest_2_ = bf16[1024,1024]{1,0:T(8,128)(2,1)} custom-call(f32[256,1024]{1,0:T(8,128)} %copy-done.23, bf16[256,1024]{1,0:T(8,128)(2,1)} %copy-done.34, bf16[256,1024]{1,0:T(8,128)(2,1)} %copy-done.35), custom_call_target="tpu_custom_call" | custom-call | flops 1 | bytes 1 | tf_op jit(solution)/shard_map/f0/gather_up/pallas_call | solution.py:136
  174.6 2.3 %gather_up.5.rest_2_ = bf16[1024,1024]{1,0:T(8,128)(2,1)} custom-call(f32[256,1024]{1,0:T(8,128)} %copy-done.22, bf16[256,1024]{1,0:T(8,128)(2,1)} %copy-done.32, bf16[256,1024]{1,0:T(8,128)(2,1)} %collective-permute-done.23.rest_1_, bf16[1024,1024]{1,0:T(8,128)(2,1)} %gather_up.4.rest_2_), custom_call_target="tpu_custom_call", output_to_operand_aliasing={{}: (3, {})} | custom-call | flops 1 | bytes 1 | tf_op jit(solution)/shard_map/f1/gather_up/pallas_call | solution.py:136
  177.7 2.3 %gather_up.6.rest_2_ = bf16[1024,1024]{1,0:T(8,128)(2,1)} custom-call(f32[256,1024]{1,0:T(8,128)} %copy-done.21, bf16[256,1024]{1,0:T(8,128)(2,1)} %copy-done.33, bf16[256,1024]{1,0:T(8,128)(2,1)} %collective-permute-done.20.rest_1_, bf16[1024,1024]{1,0:T(8,128)(2,1)} %gather_up.5.rest_2_), custom_call_target="tpu_custom_call", output_to_operand_aliasing={{}: (3, {})} | custom-call | flops 1 | bytes 1 | tf_op jit(solution)/shard_map/f2/gather_up/pallas_call | solution.py:136
  180.0 7.8 %collective-permute-done.16.rest_1_ = bf16[256,1024]{1,0:T(8,128)(2,1)} collective-permute-done((bf16[256,1024]{1,0:T(8,128)(2,1)S(1)}, bf16[256,1024]{1,0:T(8,128)(2,1)}, u32[]{:S(2)}, u32[]{:S(2)}) %collective-permute-start.16) | collective-permute-done | bytes 524320 | tf_op jit(solution)/shard_map/t32/ppermute | solution.py:329
  187.8 2.4 %gather_up.7 = bf16[1024,1024]{1,0:T(8,128)(2,1)} custom-call(f32[256,1024]{1,0:T(8,128)} %copy-done.20, bf16[256,1024]{1,0:T(8,128)(2,1)} %collective-permute-done.15.rest_0_, bf16[256,1024]{1,0:T(8,128)(2,1)} %collective-permute-done.16.rest_1_, bf16[1024,1024]{1,0:T(8,128)(2,1)} %gather_up.6.rest_2_), custom_call_target="tpu_custom_call", output_to_operand_aliasing={{}: (3, {})} | custom-call | flops 1 | bytes 1 | tf_op jit(solution)/shard_map/f3/gather_up/pallas_call | solution.py:136
  (129 shorter events, 36.6 us)
Async XLA Ops:
  0.0 36.9 %collective-permute-start.7 = (bf16[1024,8192]{1,0:T(8,128)(2,1)}, bf16[1024,8192]{1,0:T(8,128)(2,1)}, u32[]{:S(2)}, u32[]{:S(2)}) collective-permute-start(bf16[1024,8192]{1,0:T(8,128)(2,1)} %w_ref.23), channel_id=1, source_target_pairs={{0,1},{1,0},{2,3},{3,2},{4,5},{5,4},{6,7},{7,6},{8,9},{9,8},{10,11... | collective-permute-start | bytes 50331656 | tf_op jit(solution)/shard_map/ppermute | solution.py:296
  1.8 18.7 %collective-permute-start.3 = (bf16[128,1024]{1,0:T(8,128)(2,1)}, bf16[128,1024]{1,0:T(8,128)(2,1)S(1)}, u32[]{:S(2)}, u32[]{:S(2)}) collective-permute-start(bf16[128,1024]{1,0:T(8,128)(2,1)} %constant_dynamic-slice_fusion), channel_id=1, source_target_pairs={{0,8},{8,0},{16,24},{24,16},{1,9},{9,1},{17,25},{25,17},{2,10},{10... | collective-permute-start | bytes 786440 | tf_op jit(solution)/shard_map/ppermute | solution.py:292
  3.3 9.4 %collective-permute-start.4 = (bf16[128,1024]{1,0:T(8,128)(2,1)}, bf16[128,1024]{1,0:T(8,128)(2,1)S(1)}, u32[]{:S(2)}, u32[]{:S(2)}) collective-permute-start(bf16[128,1024]{1,0:T(8,128)(2,1)} %constant_dynamic-slice_fusion), channel_id=1, source_target_pairs={{0,16},{8,24},{16,0},{24,8},{1,17},{9,25},{17,1},{25,9},{2,18},{10... | collective-permute-start | bytes 786440 | tf_op jit(solution)/shard_map/ppermute | solution.py:291
  4.6 12.2 %collective-permute-start = (bf16[128,1024]{1,0:T(8,128)(2,1)}, bf16[128,1024]{1,0:T(8,128)(2,1)S(1)}, u32[]{:S(2)}, u32[]{:S(2)}) collective-permute-start(bf16[128,1024]{1,0:T(8,128)(2,1)} %constant_dynamic-slice_fusion.1), channel_id=1, source_target_pairs={{0,8},{8,0},{16,24},{24,16},{1,9},{9,1},{17,25},{25,17},{2,10},{10... | collective-permute-start | bytes 786440 | tf_op jit(solution)/shard_map/ppermute | solution.py:290
  5.1 15.5 %collective-permute-start.1 = (bf16[128,1024]{1,0:T(8,128)(2,1)}, bf16[128,1024]{1,0:T(8,128)(2,1)S(1)}, u32[]{:S(2)}, u32[]{:S(2)}) collective-permute-start(bf16[128,1024]{1,0:T(8,128)(2,1)} %constant_dynamic-slice_fusion.1), channel_id=1, source_target_pairs={{0,16},{8,24},{16,0},{24,8},{1,17},{9,25},{17,1},{25,9},{2,18},{10... | collective-permute-start | bytes 786440 | tf_op jit(solution)/shard_map/ppermute | solution.py:293
  12.7 9.1 %collective-permute-start.5 = (bf16[128,1024]{1,0:T(8,128)(2,1)S(1)}, bf16[128,1024]{1,0:T(8,128)(2,1)S(1)}, u32[]{:S(2)}, u32[]{:S(2)}) collective-permute-start(bf16[128,1024]{1,0:T(8,128)(2,1)S(1)} %collective-permute-done.4), channel_id=1, source_target_pairs={{0,8},{8,0},{16,24},{24,16},{1,9},{9,1},{17,25},{25,17},{2,10},{10... | collective-permute-start | bytes 786440 | tf_op jit(solution)/shard_map/ppermute | solution.py:295
  16.8 7.3 %collective-permute-start.2 = (bf16[128,1024]{1,0:T(8,128)(2,1)S(1)}, bf16[128,1024]{1,0:T(8,128)(2,1)}, u32[]{:S(2)}, u32[]{:S(2)}) collective-permute-start(bf16[128,1024]{1,0:T(8,128)(2,1)S(1)} %collective-permute-done), channel_id=1, source_target_pairs={{0,16},{8,24},{16,0},{24,8},{1,17},{9,25},{17,1},{25,9},{2,18},{10... | collective-permute-start | bytes 786440 | tf_op jit(solution)/shard_map/ppermute | solution.py:294
  29.7 52.1 %copy-start.2 = (bf16[256,1024]{1,0:T(8,128)(2,1)}, bf16[256,1024]{1,0:T(8,128)(2,1)S(1)}, u32[]{:S(2)}) copy-start(bf16[256,1024]{1,0:T(8,128)(2,1)S(1)} %attend.4.own_ref.refs_0_) | copy-start | bytes 1572868
  29.7 7.2 %collective-permute-start.6 = (bf16[256,1024]{1,0:T(8,128)(2,1)S(1)}, bf16[256,1024]{1,0:T(8,128)(2,1)S(1)}, u32[]{:S(2)}, u32[]{:S(2)}) collective-permute-start(bf16[256,1024]{1,0:T(8,128)(2,1)S(1)} %attend.4.own_ref.refs_0_), channel_id=1, source_target_pairs={{0,1},{1,0},{2,3},{3,2},{4,5},{5,4},{6,7},{7,6},{8,9},{9,8},{10,11... | collective-permute-start | bytes 1572872 | tf_op jit(solution)/shard_map/a0/ppermute | solution.py:309
  36.4 39.3 %copy-start.8 = (bf16[256,1024]{1,0:T(8,128)(2,1)}, bf16[256,1024]{1,0:T(8,128)(2,1)S(1)}, u32[]{:S(2)}) copy-start(bf16[256,1024]{1,0:T(8,128)(2,1)S(1)} %attend.5.refs_1_.own_ref) | copy-start | bytes 1572868
  36.4 4.2 %collective-permute-start.9 = (bf16[256,1024]{1,0:T(8,128)(2,1)S(1)}, bf16[256,1024]{1,0:T(8,128)(2,1)S(1)}, u32[]{:S(2)}, u32[]{:S(2)}) collective-permute-start(bf16[256,1024]{1,0:T(8,128)(2,1)S(1)} %attend.5.refs_1_.own_ref), channel_id=1, source_target_pairs={{0,1},{1,0},{2,3},{3,2},{4,5},{5,4},{6,7},{7,6},{8,9},{9,8},{10,11... | collective-permute-start | bytes 1572872 | tf_op jit(solution)/shard_map/a1/ppermute | solution.py:309
  36.9 44.9 %copy-start.10 = (bf16[256,1024]{1,0:T(8,128)(2,1)}, bf16[256,1024]{1,0:T(8,128)(2,1)S(1)}, u32[]{:S(2)}) copy-start(bf16[256,1024]{1,0:T(8,128)(2,1)S(1)} %collective-permute-done.6.other_ref.refs_4_) | copy-start | bytes 1572868
  39.8 12.2 %collective-permute-start.8 = (bf16[256,2048]{1,0:T(8,128)(2,1)S(1)}, bf16[256,2048]{1,0:T(8,128)(2,1)S(1)}, u32[]{:S(2)}, u32[]{:S(2)}) collective-permute-start(bf16[256,2048]{1,0:T(8,128)(2,1)S(1)} %unit.12), channel_id=1, source_target_pairs={{0,2},{7,5},{8,10},{15,13},{16,18},{23,21},{24,26},{31,29}} | collective-permute-start | bytes 3145736 | tf_op jit(solution)/shard_map/t00/ppermute | solution.py:329
  43.5 24.9 %collective-permute-start.12 = (bf16[256,2048]{1,0:T(8,128)(2,1)S(1)}, bf16[256,2048]{1,0:T(8,128)(2,1)S(1)}, u32[]{:S(2)}, u32[]{:S(2)}) collective-permute-start(bf16[256,2048]{1,0:T(8,128)(2,1)S(1)} %unit.13), channel_id=1, source_target_pairs={{0,2},{7,5},{8,10},{15,13},{16,18},{23,21},{24,26},{31,29}} | collective-permute-start | bytes 3145736 | tf_op jit(solution)/shard_map/t10/ppermute | solution.py:329
  50.8 36.4 %copy-start.6 = (bf16[256,1024]{1,0:T(8,128)(2,1)}, bf16[256,1024]{1,0:T(8,128)(2,1)S(1)}, u32[]{:S(2)}) copy-start(bf16[256,1024]{1,0:T(8,128)(2,1)S(1)} %attend.6.refs_2_.own_ref) | copy-start | bytes 1572868
  50.8 13.9 %collective-permute-start.10 = (bf16[256,1024]{1,0:T(8,128)(2,1)S(1)}, bf16[256,1024]{1,0:T(8,128)(2,1)S(1)}, u32[]{:S(2)}, u32[]{:S(2)}) collective-permute-start(bf16[256,1024]{1,0:T(8,128)(2,1)S(1)} %attend.6.refs_2_.own_ref), channel_id=1, source_target_pairs={{0,1},{1,0},{2,3},{3,2},{4,5},{5,4},{6,7},{7,6},{8,9},{9,8},{10,11... | collective-permute-start | bytes 1572872 | tf_op jit(solution)/shard_map/a2/ppermute | solution.py:309
  59.5 10.6 %collective-permute-start.11 = (bf16[256,1024]{1,0:T(8,128)(2,1)S(1)}, bf16[256,1024]{1,0:T(8,128)(2,1)S(1)}, u32[]{:S(2)}, u32[]{:S(2)}) collective-permute-start(bf16[256,1024]{1,0:T(8,128)(2,1)S(1)} %attend.7.refs_3_.own_ref), channel_id=1, source_target_pairs={{0,1},{1,0},{2,3},{3,2},{4,5},{5,4},{6,7},{7,6},{8,9},{9,8},{10,11... | collective-permute-start | bytes 1572872 | tf_op jit(solution)/shard_map/a3/ppermute | solution.py:309
  68.5 18.7 %collective-permute-start.17 = (bf16[256,2048]{1,0:T(8,128)(2,1)}, bf16[256,2048]{1,0:T(8,128)(2,1)}, u32[]{:S(2)}, u32[]{:S(2)}) collective-permute-start(bf16[256,2048]{1,0:T(8,128)(2,1)} %unit.17), channel_id=1, source_target_pairs={{0,2},{7,5},{8,10},{15,13},{16,18},{23,21},{24,26},{31,29}} | collective-permute-start | bytes 3145736 | tf_op jit(solution)/shard_map/t20/ppermute | solution.py:329
  73.9 18.4 %collective-permute-start.13 = (bf16[256,2048]{1,0:T(8,128)(2,1)}, bf16[256,2048]{1,0:T(8,128)(2,1)}, u32[]{:S(2)}, u32[]{:S(2)}) collective-permute-start(bf16[256,2048]{1,0:T(8,128)(2,1)} %unit.14), channel_id=1, source_target_pairs={{0,2},{7,5},{8,10},{15,13},{16,18},{23,21},{24,26},{31,29}} | collective-permute-start | bytes 3145736 | tf_op jit(solution)/shard_map/t30/ppermute | solution.py:329
  80.5 27.9 %collective-permute-start.21 = (bf16[256,2048]{1,0:T(8,128)(2,1)}, bf16[256,2048]{1,0:T(8,128)(2,1)}, u32[]{:S(2)}, u32[]{:S(2)}) collective-permute-start(bf16[256,2048]{1,0:T(8,128)(2,1)} %unit.20), channel_id=1, source_target_pairs={{0,2},{7,5},{2,4},{5,3},{8,10},{15,13},{10,12},{13,11},{16,18},{23... | collective-permute-start | bytes 3145736 | tf_op jit(solution)/shard_map/t11/ppermute | solution.py:329
  85.7 30.5 %collective-permute-start.24 = (bf16[256,2048]{1,0:T(8,128)(2,1)}, bf16[256,2048]{1,0:T(8,128)(2,1)}, u32[]{:S(2)}, u32[]{:S(2)}) collective-permute-start(bf16[256,2048]{1,0:T(8,128)(2,1)} %unit.22), channel_id=1, source_target_pairs={{0,2},{7,5},{2,4},{5,3},{8,10},{15,13},{10,12},{13,11},{16,18},{23... | collective-permute-start | bytes 3145736 | tf_op jit(solution)/shard_map/t01/ppermute | solution.py:329
  91.0 54.0 %collective-permute-start.18 = (bf16[256,2048]{1,0:T(8,128)(2,1)}, bf16[256,2048]{1,0:T(8,128)(2,1)S(1)}, u32[]{:S(2)}, u32[]{:S(2)}) collective-permute-start(bf16[256,2048]{1,0:T(8,128)(2,1)} %unit.18), channel_id=1, source_target_pairs={{0,2},{7,5},{2,4},{5,3},{8,10},{15,13},{10,12},{13,11},{16,18},{23... | collective-permute-start | bytes 3145736 | tf_op jit(solution)/shard_map/t21/ppermute | solution.py:329
  95.4 58.3 %collective-permute-start.14 = (bf16[256,2048]{1,0:T(8,128)(2,1)S(1)}, bf16[256,2048]{1,0:T(8,128)(2,1)}, u32[]{:S(2)}, u32[]{:S(2)}) collective-permute-start(bf16[256,2048]{1,0:T(8,128)(2,1)S(1)} %unit.15), channel_id=1, source_target_pairs={{0,2},{7,5},{2,4},{5,3},{8,10},{15,13},{10,12},{13,11},{16,18},{23... | collective-permute-start | bytes 3145736 | tf_op jit(solution)/shard_map/t31/ppermute | solution.py:329
  114.1 34.0 %copy-start.7 = (bf16[256,1024]{1,0:T(8,128)(2,1)S(1)}, bf16[256,1024]{1,0:T(8,128)(2,1)}, u32[]{:S(2)}) copy-start(bf16[256,1024]{1,0:T(8,128)(2,1)} %copy-done.6) | copy-start | bytes 1572868
  114.1 47.3 %collective-permute-start.22 = (bf16[256,1024]{1,0:T(8,128)(2,1)S(1)}, bf16[256,1024]{1,0:T(8,128)(2,1)S(1)}, u32[]{:S(2)}, u32[]{:S(2)}) collective-permute-start(bf16[256,1024]{1,0:T(8,128)(2,1)S(1)} %get-tuple-element.35), channel_id=1, source_target_pairs={{0,2},{7,5},{2,4},{5,3},{4,6},{3,1},{8,10},{15,13},{10,12},{13,11}... | collective-permute-start | bytes 1572872 | tf_op jit(solution)/shard_map/t12/ppermute | solution.py:329
  121.8 42.7 %collective-permute-start.25 = (bf16[256,1024]{1,0:T(8,128)(2,1)S(1)}, bf16[256,1024]{1,0:T(8,128)(2,1)S(1)}, u32[]{:S(2)}, u32[]{:S(2)}) collective-permute-start(bf16[256,1024]{1,0:T(8,128)(2,1)S(1)} %get-tuple-element.39), channel_id=1, source_target_pairs={{0,2},{7,5},{2,4},{5,3},{4,6},{3,1},{8,10},{15,13},{10,12},{13,11}... | collective-permute-start | bytes 1572872 | tf_op jit(solution)/shard_map/t02/ppermute | solution.py:329
  123.7 42.8 %collective-permute-start.26 = (bf16[256,1024]{1,0:T(8,128)(2,1)S(1)}, bf16[256,1024]{1,0:T(8,128)(2,1)S(1)}, u32[]{:S(2)}, u32[]{:S(2)}) collective-permute-start(bf16[256,1024]{1,0:T(8,128)(2,1)S(1)} %get-tuple-element.40), channel_id=1, source_target_pairs={{0,3},{7,4},{2,5},{5,2},{4,7},{3,0},{8,11},{15,12},{10,13},{13,10}... | collective-permute-start | bytes 1572872 | tf_op jit(solution)/shard_map/t02/ppermute | solution.py:329
  146.1 28.5 %collective-permute-start.23 = (bf16[256,1024]{1,0:T(8,128)(2,1)S(1)}, bf16[256,1024]{1,0:T(8,128)(2,1)}, u32[]{:S(2)}, u32[]{:S(2)}) collective-permute-start(bf16[256,1024]{1,0:T(8,128)(2,1)S(1)} %get-tuple-element.36), channel_id=1, source_target_pairs={{0,3},{7,4},{2,5},{5,2},{4,7},{3,0},{8,11},{15,12},{10,13},{13,10}... | collective-permute-start | bytes 1572872 | tf_op jit(solution)/shard_map/t12/ppermute | solution.py:329
  153.7 23.2 %collective-permute-start.19 = (bf16[256,1024]{1,0:T(8,128)(2,1)S(1)}, bf16[256,1024]{1,0:T(8,128)(2,1)S(1)}, u32[]{:S(2)}, u32[]{:S(2)}) collective-permute-start(bf16[256,1024]{1,0:T(8,128)(2,1)S(1)} %get-tuple-element.32), channel_id=1, source_target_pairs={{0,2},{7,5},{2,4},{5,3},{4,6},{3,1},{8,10},{15,13},{10,12},{13,11}... | collective-permute-start | bytes 1572872 | tf_op jit(solution)/shard_map/t22/ppermute | solution.py:329
  161.5 15.4 %collective-permute-start.20 = (bf16[256,1024]{1,0:T(8,128)(2,1)S(1)}, bf16[256,1024]{1,0:T(8,128)(2,1)}, u32[]{:S(2)}, u32[]{:S(2)}) collective-permute-start(bf16[256,1024]{1,0:T(8,128)(2,1)S(1)} %get-tuple-element.33), channel_id=1, source_target_pairs={{0,3},{7,4},{2,5},{5,2},{4,7},{3,0},{8,11},{15,12},{10,13},{13,10}... | collective-permute-start | bytes 1572872 | tf_op jit(solution)/shard_map/t22/ppermute | solution.py:329
  164.5 15.4 %collective-permute-start.15 = (bf16[256,1024]{1,0:T(8,128)(2,1)S(1)}, bf16[256,1024]{1,0:T(8,128)(2,1)}, u32[]{:S(2)}, u32[]{:S(2)}) collective-permute-start(bf16[256,1024]{1,0:T(8,128)(2,1)S(1)} %get-tuple-element.28), channel_id=1, source_target_pairs={{0,2},{7,5},{2,4},{5,3},{4,6},{3,1},{8,10},{15,13},{10,12},{13,11}... | collective-permute-start | bytes 1572872 | tf_op jit(solution)/shard_map/t32/ppermute | solution.py:329
  167.3 20.5 %collective-permute-start.16 = (bf16[256,1024]{1,0:T(8,128)(2,1)S(1)}, bf16[256,1024]{1,0:T(8,128)(2,1)}, u32[]{:S(2)}, u32[]{:S(2)}) collective-permute-start(bf16[256,1024]{1,0:T(8,128)(2,1)S(1)} %get-tuple-element.29), channel_id=1, source_target_pairs={{0,3},{7,4},{2,5},{5,2},{4,7},{3,0},{8,11},{15,12},{10,13},{13,10}... | collective-permute-start | bytes 1572872 | tf_op jit(solution)/shard_map/t32/ppermute | solution.py:329
  (31 other events, 227.4 us)

commit v2 on v1

--- a/solution.py
+++ b/solution.py
@@ -21,7 +21,8 @@
 def attend_kernel(
     row_tile, block_len, held, heads, n_pieces, scal, q_ref, *rest
 ):
-    pieces, (o_ref, kv, acc, top, sem) = rest[:n_pieces], rest[n_pieces:]
+    pieces, outs = rest[:n_pieces], rest[n_pieces:-4]
+    kv, acc, top, sem = rest[-4:]
     tile = pl.program_id(0)
     n_own = kv.shape[0]
     n_tiles_all, n_blocks = held
@@ -83,11 +84,15 @@
         return carry
 
     lax.fori_loop(low // TK, (place + TQ - 1) // TK + 1, one, 0)
-    for h in range(heads):
-        o_ref[:, h * HD : (h + 1) * HD] = (acc[h, :, 0:HD] / acc[h, :, HD:]).astype(o_ref.dtype)
-
-
-def attend(scal, queries, pieces, row_tile, n_rows, n_blocks, block_len, n_own):
+    for n, out in enumerate(outs):
+
+        @pl.when((len(outs) == 1) | (tile == n))
+        def _():
+            for h in range(heads):
+                out[:, h * HD : (h + 1) * HD] = (acc[h, :, 0:HD] / acc[h, :, HD:]).astype(out.dtype)
+
+
+def attend(scal, queries, pieces, row_tile, n_rows, n_blocks, block_len, n_own, n_out=1):
     width = queries.shape[1]
     heads = width // HD
     tiles_all = queries.shape[0] // TQ
@@ -96,13 +101,13 @@
         functools.partial(
             attend_kernel, row_tile, block_len, (tiles_all, n_blocks), heads, len(pieces)
         ),
-        out_shape=jax.ShapeDtypeStruct((n_rows, width), jnp.bfloat16),
+        out_shape=[jax.ShapeDtypeStruct((n_rows // n_out, width), jnp.bfloat16)] * n_out,
         grid_spec=pltpu.PrefetchScalarGridSpec(
             num_scalar_prefetch=1,
             grid=(n_rows // TQ,),
             in_specs=[pl.BlockSpec((TQ, width), lambda i, s: (row_tile + i, 0))]
             + [pl.BlockSpec(memory_space=pltpu.HBM)] * len(pieces),
-            out_specs=pl.BlockSpec((TQ, width), lambda i, s: (i, 0)),
+            out_specs=[pl.BlockSpec((TQ, width), lambda i, s: (i if n_out == 1 else 0, 0))] * n_out,
             scratch_shapes=[
                 pltpu.VMEM((n_own, 3 * HD, tokens), jnp.bfloat16),
                 pltpu.VMEM((heads, TQ, 2 * HD), jnp.float32),
@@ -252,7 +257,7 @@
     block_len = doc_ids.shape[0] // n_blocks
     gathered = [lax.all_gather(own_head(a), "ctx", axis=0) for a in (key_heads, value_heads)]
     scal = tables(block_order, doc_ids, row_count, jnp.arange(n_own, dtype=jnp.int32))
-    context = attend(scal, queries, gathered, 0, row_count, n_blocks, block_len, n_own)
+    context = attend(scal, queries, gathered, 0, row_count, n_blocks, block_len, n_own)[0]
     partial_sum = jnp.dot(context, out_weight, preferred_element_type=jnp.float32)
     return lax.psum_scatter(
         partial_sum.astype(jnp.bfloat16), "head", scatter_dimension=1, tiled=True
@@ -269,9 +274,9 @@
 
 
 def named(step, name):
-    def run(*args):
+    def run(*args, **kw):
         with jax.named_scope(name + "".join(str(a) for a in args if isinstance(a, int))):
-            return step(*args)
+            return step(*args, **kw)
 
     return run
 
@@ -302,11 +307,14 @@
 
     chunks = row_count // CHUNK
     mine, other, base, received = {}, {}, {}, {}
-    def attention(k, *behind):
-        mine[k] = attend(
-            tied(scal, *behind), queries, pieces, k * CHUNK // TQ, CHUNK, n_blocks, block_len, 4
+    def attention(k, *behind, count=1):
+        found = attend(
+            tied(scal, *behind), queries, pieces, k * CHUNK // TQ, count * CHUNK, n_blocks,
+            block_len, 4, count,
         )
-        other[k] = lax.ppermute(mine[k], "head", swap)
+        for n in range(count):
+            mine[k + n] = found[n]
+            other[k + n] = lax.ppermute(found[n], "head", swap)
 
     def tick(k, s, *behind):
         valid = (far <= s) & (far <= 2)
@@ -348,9 +356,8 @@
     attention(0)
     attention(1, mine[0])
     tick(0, 0)
-    attention(2, mine[1], sent[0, 0][0])
     tick(1, 0)
-    attention(3, mine[2], received[0, 0][0])
+    attention(2, mine[1], sent[1, 0][0], count=2)
     tick(2, 0, received[0, 0][0])
     tick(3, 0, received[1, 0][0])
     for s in (1, 2):

time: 192 us -> 190 us (0.990); the launches traced: 190 us -> 190 us
  waiting for transfers between devices: 19.3 us -> 22.8 us
  local copies, waits for them, and re-layouts: 11.6 us -> 8.85 us
    ppermute x16, starting transfers between devices: 49.5 us -> 55.1 us  [tick(): lax.ppermute(sent[k, s][cross], 'head', pairs)]
    ppermute x4, starting transfers between devices: 7.01 us -> 1.95 us  [attention(): other[k + n] = lax.ppermute(found[n], 'head', swap)]
    unnamed x72 -> x68, local copies, waits for them, and re-layouts: 6.63 us -> 3.83 us
    ppermute x16, waiting for transfers between devices: 7.83 us -> 9.94 us  [tick(): lax.ppermute(sent[k, s][cross], 'head', pairs)]
    pallas_call x4 -> x3, Pallas kernels: 26 us -> 24.9 us  [attend(): pl.pallas_call(functools.partial(attend_kernel, row_tile, block_len, (til...]
  transfers between devices with their start and end apart: 27 -> 27, of which waited for: 5 -> 7; matrix products, arithmetic and copies ran while one was open for 4% -> 4% of each run, Pallas kernels for 48% -> 48%
where the time goes in v2:
time: 190 us
  Pallas kernels  93.2 us (49%)
  starting transfers between devices  62.1 us (33%)
  waiting for transfers between devices  22.8 us (12%)
  local copies, waits for them, and re-layouts  8.85 us (5%)
  other arithmetic  2.8 us (1%)
    ppermute x16, starting transfers between devices, tick(): lax.ppermute(sent[k, s][cross], 'head', pairs)  55.1 us
    pallas_call x12, Pallas kernels, unit(): pl.pallas_call(functools.partial(unit_kernel, len(adds), n_out), out_shap...  50.4 us
    pallas_call x3, Pallas kernels, attend(): pl.pallas_call(functools.partial(attend_kernel, row_tile, block_len, (til...  24.9 us
    ppermute x16, waiting for transfers between devices, tick(): lax.ppermute(sent[k, s][cross], 'head', pairs)  9.94 us
    pallas_call x4, Pallas kernels, gather_up(): pl.pallas_call(gather_kernel, out_shape=jax.ShapeDtypeStruct((total_rows,...  9.34 us
    pallas_call x1, Pallas kernels, own_product(): pl.pallas_call(functools.partial(own_kernel, n), out_shape=[jax.ShapeDtyp...  8.52 us
    ppermute x1, waiting for transfers between devices, line(): values_2 = lax.ppermute(values, 'ctx', along[1])  4.35 us
    unnamed x68, local copies, waits for them, and re-layouts  3.83 us
  transfers between devices with their start and end apart: 27, of which 7 were waited for; matrix products, arithmetic and copies ran while one was open for 4% of the time, Pallas kernels for 48%

profile of v2, /device:TPU:20, one launch (start us, length us, event | category | flops | bytes accessed | tf_op | source)
XLA Modules:
  0.0 190.4 jit_solution(10729513896690875686)
XLA Ops:
  8.3 4.3 %collective-permute-done.4 = bf16[128,1024]{1,0:T(8,128)(2,1)S(1)} collective-permute-done((bf16[128,1024]{1,0:T(8,128)(2,1)}, bf16[128,1024]{1,0:T(8,128)(2,1)S(1)}, u32[]{:S(2)}, u32[]{:S(2)}) %collective-permute-start.4) | collective-permute-done | bytes 262176 | tf_op jit(solution)/shard_map/ppermute | solution.py:296
  13.2 3.5 %collective-permute-done = bf16[128,1024]{1,0:T(8,128)(2,1)S(1)} collective-permute-done((bf16[128,1024]{1,0:T(8,128)(2,1)}, bf16[128,1024]{1,0:T(8,128)(2,1)S(1)}, u32[]{:S(2)}, u32[]{:S(2)}) %collective-permute-start) | collective-permute-done | bytes 262176 | tf_op jit(solution)/shard_map/ppermute | solution.py:295
  21.8 2.2 %collective-permute-done.2 = bf16[128,1024]{1,0:T(8,128)(2,1)} collective-permute-done((bf16[128,1024]{1,0:T(8,128)(2,1)S(1)}, bf16[128,1024]{1,0:T(8,128)(2,1)}, u32[]{:S(2)}, u32[]{:S(2)}) %collective-permute-start.2) | collective-permute-done | bytes 262176 | tf_op jit(solution)/shard_map/ppermute | solution.py:299
  24.1 7.5 %attend.3.refs_0_.own_ref = bf16[256,1024]{1,0:T(8,128)(2,1)S(1)} custom-call(s32[22]{0:T(128)S(1)} %concatenate.3.scal, bf16[1024,1024]{1,0:T(8,128)(2,1)} %q_ref.5, bf16[1,128,1024]{2,1,0:T(8,128)(2,1)} %fusion.2.rest_0_, bf16[1,128,1024]{2,1,0:T(8,128)(2,1)} %bitcast.28, bf16[1,128,1024]{2,1,0:T(8,128)(2,1)} %bitcast.31, ...), custom_call_target="tpu_custom_call" | custom-call | flops 1 | bytes 1 | tf_op jit(solution)/shard_map/a0/attend/pallas_call | solution.py:100
  31.7 8.4 %attend.4.own_ref.refs_1_ = bf16[256,1024]{1,0:T(8,128)(2,1)S(1)} custom-call(s32[22]{0:T(128)S(1)} %concatenate.3.scal, bf16[1024,1024]{1,0:T(8,128)(2,1)} %q_ref.5, bf16[1,128,1024]{2,1,0:T(8,128)(2,1)} %fusion.2.rest_0_, bf16[1,128,1024]{2,1,0:T(8,128)(2,1)} %bitcast.29, bf16[1,128,1024]{2,1,0:T(8,128)(2,1)} %bitcast.32, ...), custom_call_target="tpu_custom_call" | custom-call | flops 1 | bytes 1 | tf_op jit(solution)/shard_map/a1/attend/pallas_call | solution.py:100
  40.8 2.9 %unit.16 = bf16[256,2048]{1,0:T(8,128)(2,1)S(1)} custom-call(s32[3]{0:T(128)S(1)} %add_add_fusion.scal, bf16[256,1024]{1,0:T(8,128)(2,1)S(1)} %attend.3.refs_0_.own_ref, bf16[256,1024]{1,0:T(8,128)(2,1)S(1)} %collective-permute-done.8.refs_4_.other_ref, bf16[1024,8192]{1,0:T(8,128)(2,1)} %w_ref.23, bf16[1024,8192]{1,0:T(8,128)(2,1)} %collective-permute-done.7.wp_ref.refs_9_), custom_call_target="tpu_custom_call" | custom-call | flops 1 | bytes 1 | tf_op jit(solution)/shard_map/t00/unit/pallas_call | solution.py:189
  44.5 2.9 %unit.12 = bf16[256,2048]{1,0:T(8,128)(2,1)S(1)} custom-call(s32[3]{0:T(128)S(1)} %add_add_fusion.scal, bf16[256,1024]{1,0:T(8,128)(2,1)S(1)} %attend.4.own_ref.refs_1_, bf16[256,1024]{1,0:T(8,128)(2,1)S(1)} %collective-permute-done.6.other_ref.refs_5_, bf16[1024,8192]{1,0:T(8,128)(2,1)} %w_ref.23, bf16[1024,8192]{1,0:T(8,128)(2,1)} %collective-permute-done.7.wp_ref.refs_9_), custom_call_target="tpu_custom_call" | custom-call | flops 1 | bytes 1 | tf_op jit(solution)/shard_map/t10/unit/pallas_call | solution.py:189
  48.1 9.0 %attend.5 = (bf16[256,1024]{1,0:T(8,128)(2,1)S(1)}, bf16[256,1024]{1,0:T(8,128)(2,1)S(1)}) custom-call(s32[22]{0:T(128)S(1)} %concatenate.3.scal, bf16[1024,1024]{1,0:T(8,128)(2,1)} %q_ref.5, bf16[1,128,1024]{2,1,0:T(8,128)(2,1)} %fusion.2.rest_0_, bf16[1,128,1024]{2,1,0:T(8,128)(2,1)} %bitcast.30, bf16[1,128,1024]{2,1,0:T(8,128)(2,1)} %bitcast.33, ...), custom_call_target="tpu_custom_call" | custom-call | flops 1 | bytes 1 | tf_op jit(solution)/shard_map/a2/attend/pallas_call | solution.py:100
  59.9 3.8 %unit.17 = bf16[256,2048]{1,0:T(8,128)(2,1)} custom-call(s32[3]{0:T(128)S(1)} %add_add_fusion.scal, bf16[256,1024]{1,0:T(8,128)(2,1)S(1)} %get-tuple-element.26.refs_2_.own_ref, bf16[256,1024]{1,0:T(8,128)(2,1)S(1)} %collective-permute-done.9.refs_6_.other_ref, bf16[1024,8192]{1,0:T(8,128)(2,1)} %w_ref.23, ...), custom_call_target="tpu_custom_call" | custom-call | flops 1 | bytes 1 | tf_op jit(solution)/shard_map/t20/unit/pallas_call | solution.py:189
  65.5 3.8 %unit.13 = bf16[256,2048]{1,0:T(8,128)(2,1)} custom-call(s32[3]{0:T(128)S(1)} %add_add_fusion.scal, bf16[256,1024]{1,0:T(8,128)(2,1)S(1)} %get-tuple-element.27.refs_3_.own_ref, bf16[256,1024]{1,0:T(8,128)(2,1)S(1)} %collective-permute-done.10.refs_7_.other_ref, bf16[1024,8192]{1,0:T(8,128)(2,1)} %w_ref.23, ...), custom_call_target="tpu_custom_call" | custom-call | flops 1 | bytes 1 | tf_op jit(solution)/shard_map/t30/unit/pallas_call | solution.py:189
  71.0 3.9 %unit.20 = bf16[256,2048]{1,0:T(8,128)(2,1)} custom-call(s32[3]{0:T(128)S(1)} %add_add_fusion.2.scal, bf16[256,1024]{1,0:T(8,128)(2,1)S(1)} %attend.4.own_ref.refs_1_, bf16[256,1024]{1,0:T(8,128)(2,1)S(1)} %collective-permute-done.6.other_ref.refs_5_, bf16[1024,8192]{1,0:T(8,128)(2,1)} %w_ref.23, bf16[1024,8192]{1,0:T(8,128)(2,1)} %collective-permute-done.7.wp_ref.refs_9_, ...), custom_call_target="tpu_custom_call" | custom-call | flops 1 | bytes 1 | tf_op jit(solution)/shard_map/t11/unit/pallas_call | solution.py:189
  76.5 3.9 %unit.22 = bf16[256,2048]{1,0:T(8,128)(2,1)} custom-call(s32[3]{0:T(128)S(1)} %add_add_fusion.2.scal, bf16[256,1024]{1,0:T(8,128)(2,1)S(1)} %attend.3.refs_0_.own_ref, bf16[256,1024]{1,0:T(8,128)(2,1)S(1)} %collective-permute-done.8.refs_4_.other_ref, bf16[1024,8192]{1,0:T(8,128)(2,1)} %w_ref.23, bf16[1024,8192]{1,0:T(8,128)(2,1)} %collective-permute-done.7.wp_ref.refs_9_, ...), custom_call_target="tpu_custom_call" | custom-call | flops 1 | bytes 1 | tf_op jit(solution)/shard_map/t01/unit/pallas_call | solution.py:189
  81.8 3.9 %unit.18 = bf16[256,2048]{1,0:T(8,128)(2,1)} custom-call(s32[3]{0:T(128)S(1)} %add_add_fusion.2.scal, bf16[256,1024]{1,0:T(8,128)(2,1)S(1)} %get-tuple-element.26.refs_2_.own_ref, bf16[256,1024]{1,0:T(8,128)(2,1)S(1)} %copy-done.18, bf16[1024,8192]{1,0:T(8,128)(2,1)} %w_ref.23, bf16[1024,8192]{1,0:T(8,128)(2,1)} %collective-permute-done.7.wp_ref.refs_9_, ...), custom_call_target="tpu_custom_call" | custom-call | flops 1 | bytes 1 | tf_op jit(solution)/shard_map/t21/unit/pallas_call | solution.py:189
  87.0 3.0 %unit.14 = bf16[256,2048]{1,0:T(8,128)(2,1)S(1)} custom-call(s32[3]{0:T(128)S(1)} %add_add_fusion.2.scal, bf16[256,1024]{1,0:T(8,128)(2,1)S(1)} %get-tuple-element.27.refs_3_.own_ref, bf16[256,1024]{1,0:T(8,128)(2,1)S(1)} %copy-done.15, bf16[1024,8192]{1,0:T(8,128)(2,1)} %w_ref.23, bf16[1024,8192]{1,0:T(8,128)(2,1)} %collective-permute-done.7.wp_ref.refs_9_, ...), custom_call_target="tpu_custom_call" | custom-call | flops 1 | bytes 1 | tf_op jit(solution)/shard_map/t31/unit/pallas_call | solution.py:189
  91.6 8.5 %own_product.1 = (f32[256,1024]{1,0:T(8,128)S(1)}, f32[256,1024]{1,0:T(8,128)S(1)}, f32[256,1024]{1,0:T(8,128)S(1)}, f32[256,1024]{1,0:T(8,128)S(1)}) custom-call(s32[3]{0:T(128)S(1)} %pad_add_fusion.scal, bf16[256,1024]{1,0:T(8,128)(2,1)} %copy-done.2, bf16[256,1024]{1,0:T(8,128)(2,1)} %copy-done.4, bf16[256,1024]{1,0:T(8,128)(2,1)} %copy-done.12, ...), custom_call_target="tpu_custom_call" | custom-call | flops 1 | bytes 1 | tf_op jit(solution)/shard_map/o/own_product/pallas_call | solution.py:218
  103.1 5.6 %unit.21 = (bf16[256,1024]{1,0:T(8,128)(2,1)S(1)}, bf16[256,1024]{1,0:T(8,128)(2,1)S(1)}) custom-call(s32[3]{0:T(128)S(1)} %add_add_fusion.1.scal, bf16[256,1024]{1,0:T(8,128)(2,1)S(1)} %copy-done.5, bf16[256,1024]{1,0:T(8,128)(2,1)S(1)} %copy-done.9, bf16[1024,8192]{1,0:T(8,128)(2,1)} %w_ref.23, bf16[1024,8192]{1,0:T(8,128)(2,1)} %collective-permute-done.7.wp_ref.refs_9_, ...), custom_call_target="tpu_custom_call" | custom-call | flops 1 | bytes 1 | tf_op jit(solution)/shard_map/t12/unit/pallas_call | solution.py:189
  108.7 7.2 %collective-permute-start.22 = (bf16[256,1024]{1,0:T(8,128)(2,1)S(1)}, bf16[256,1024]{1,0:T(8,128)(2,1)S(1)}, u32[]{:S(2)}, u32[]{:S(2)}) collective-permute-start(bf16[256,1024]{1,0:T(8,128)(2,1)S(1)} %get-tuple-element.37), channel_id=1, source_target_pairs={{0,2},{7,5},{2,4},{5,3},{4,6},{3,1},{8,10},{15,13},{10,12},{13,11}... | collective-permute-start | bytes 1572872 | tf_op jit(solution)/shard_map/t12/ppermute | solution.py:337
  116.0 5.5 %unit.23 = (bf16[256,1024]{1,0:T(8,128)(2,1)S(1)}, bf16[256,1024]{1,0:T(8,128)(2,1)S(1)}) custom-call(s32[3]{0:T(128)S(1)} %add_add_fusion.1.scal, bf16[256,1024]{1,0:T(8,128)(2,1)S(1)} %copy-done.3, bf16[256,1024]{1,0:T(8,128)(2,1)S(1)} %copy-done.7, bf16[1024,8192]{1,0:T(8,128)(2,1)} %w_ref.23, bf16[1024,8192]{1,0:T(8,128)(2,1)} %collective-permute-done.7.wp_ref.refs_9_, ...), custom_call_target="tpu_custom_call" | custom-call | flops 1 | bytes 1 | tf_op jit(solution)/shard_map/t02/unit/pallas_call | solution.py:189
  121.5 1.9 %collective-permute-start.25 = (bf16[256,1024]{1,0:T(8,128)(2,1)S(1)}, bf16[256,1024]{1,0:T(8,128)(2,1)S(1)}, u32[]{:S(2)}, u32[]{:S(2)}) collective-permute-start(bf16[256,1024]{1,0:T(8,128)(2,1)S(1)} %get-tuple-element.41), channel_id=1, source_target_pairs={{0,2},{7,5},{2,4},{5,3},{4,6},{3,1},{8,10},{15,13},{10,12},{13,11}... | collective-permute-start | bytes 1572872 | tf_op jit(solution)/shard_map/t02/ppermute | solution.py:337
  123.5 21.6 %collective-permute-start.26 = (bf16[256,1024]{1,0:T(8,128)(2,1)S(1)}, bf16[256,1024]{1,0:T(8,128)(2,1)S(1)}, u32[]{:S(2)}, u32[]{:S(2)}) collective-permute-start(bf16[256,1024]{1,0:T(8,128)(2,1)S(1)} %get-tuple-element.42), channel_id=1, source_target_pairs={{0,3},{7,4},{2,5},{5,2},{4,7},{3,0},{8,11},{15,12},{10,13},{13,10}... | collective-permute-start | bytes 1572872 | tf_op jit(solution)/shard_map/t02/ppermute | solution.py:337
  145.2 2.1 %collective-permute-start.23 = (bf16[256,1024]{1,0:T(8,128)(2,1)S(1)}, bf16[256,1024]{1,0:T(8,128)(2,1)}, u32[]{:S(2)}, u32[]{:S(2)}) collective-permute-start(bf16[256,1024]{1,0:T(8,128)(2,1)S(1)} %get-tuple-element.38), channel_id=1, source_target_pairs={{0,3},{7,4},{2,5},{5,2},{4,7},{3,0},{8,11},{15,12},{10,13},{13,10}... | collective-permute-start | bytes 1572872 | tf_op jit(solution)/shard_map/t12/ppermute | solution.py:337
  147.2 5.5 %unit.19 = (bf16[256,1024]{1,0:T(8,128)(2,1)S(1)}, bf16[256,1024]{1,0:T(8,128)(2,1)S(1)}) custom-call(s32[3]{0:T(128)S(1)} %add_add_fusion.1.scal, bf16[256,1024]{1,0:T(8,128)(2,1)S(1)} %copy-done.13, bf16[256,1024]{1,0:T(8,128)(2,1)S(1)} %copy-done.19, bf16[1024,8192]{1,0:T(8,128)(2,1)} %w_ref.23, bf16[1024,8192]{1,0:T(8,128)(2,1)} %collective-permute-done.7.wp_ref.refs_9_, ...), custom_call_target="tpu_custom_call" | custom-call | flops 1 | bytes 1 | tf_op jit(solution)/shard_map/t22/unit/pallas_call | solution.py:189
  152.8 1.9 %collective-permute-start.19 = (bf16[256,1024]{1,0:T(8,128)(2,1)S(1)}, bf16[256,1024]{1,0:T(8,128)(2,1)}, u32[]{:S(2)}, u32[]{:S(2)}) collective-permute-start(bf16[256,1024]{1,0:T(8,128)(2,1)S(1)} %get-tuple-element.34), channel_id=1, source_target_pairs={{0,2},{7,5},{2,4},{5,3},{4,6},{3,1},{8,10},{15,13},{10,12},{13,11}... | collective-permute-start | bytes 1572872 | tf_op jit(solution)/shard_map/t22/ppermute | solution.py:337
  154.7 5.5 %unit.15 = (bf16[256,1024]{1,0:T(8,128)(2,1)S(1)}, bf16[256,1024]{1,0:T(8,128)(2,1)S(1)}) custom-call(s32[3]{0:T(128)S(1)} %add_add_fusion.1.scal, bf16[256,1024]{1,0:T(8,128)(2,1)S(1)} %copy-done.11, bf16[256,1024]{1,0:T(8,128)(2,1)S(1)} %copy-done.16, bf16[1024,8192]{1,0:T(8,128)(2,1)} %w_ref.23, bf16[1024,8192]{1,0:T(8,128)(2,1)} %collective-permute-done.7.wp_ref.refs_9_, ...), custom_call_target="tpu_custom_call" | custom-call | flops 1 | bytes 1 | tf_op jit(solution)/shard_map/t32/unit/pallas_call | solution.py:189
  160.3 3.8 %collective-permute-start.20 = (bf16[256,1024]{1,0:T(8,128)(2,1)S(1)}, bf16[256,1024]{1,0:T(8,128)(2,1)}, u32[]{:S(2)}, u32[]{:S(2)}) collective-permute-start(bf16[256,1024]{1,0:T(8,128)(2,1)S(1)} %get-tuple-element.35), channel_id=1, source_target_pairs={{0,3},{7,4},{2,5},{5,2},{4,7},{3,0},{8,11},{15,12},{10,13},{13,10}... | collective-permute-start | bytes 1572872 | tf_op jit(solution)/shard_map/t22/ppermute | solution.py:337
  164.1 1.9 %collective-permute-start.14 = (bf16[256,1024]{1,0:T(8,128)(2,1)S(1)}, bf16[256,1024]{1,0:T(8,128)(2,1)}, u32[]{:S(2)}, u32[]{:S(2)}) collective-permute-start(bf16[256,1024]{1,0:T(8,128)(2,1)S(1)} %get-tuple-element.30), channel_id=1, source_target_pairs={{0,2},{7,5},{2,4},{5,3},{4,6},{3,1},{8,10},{15,13},{10,12},{13,11}... | collective-permute-start | bytes 1572872 | tf_op jit(solution)/shard_map/t32/ppermute | solution.py:337
  166.9 4.2 %collective-permute-start.15 = (bf16[256,1024]{1,0:T(8,128)(2,1)S(1)}, bf16[256,1024]{1,0:T(8,128)(2,1)}, u32[]{:S(2)}, u32[]{:S(2)}) collective-permute-start(bf16[256,1024]{1,0:T(8,128)(2,1)S(1)} %get-tuple-element.31), channel_id=1, source_target_pairs={{0,3},{7,4},{2,5},{5,2},{4,7},{3,0},{8,11},{15,12},{10,13},{13,10}... | collective-permute-start | bytes 1572872 | tf_op jit(solution)/shard_map/t32/ppermute | solution.py:337
  171.1 2.3 %gather_up.4.rest_2_ = bf16[1024,1024]{1,0:T(8,128)(2,1)} custom-call(f32[256,1024]{1,0:T(8,128)} %copy-done.23, bf16[256,1024]{1,0:T(8,128)(2,1)} %copy-done.32, bf16[256,1024]{1,0:T(8,128)(2,1)} %copy-done.33), custom_call_target="tpu_custom_call" | custom-call | flops 1 | bytes 1 | tf_op jit(solution)/shard_map/f0/gather_up/pallas_call | solution.py:141
  173.5 2.3 %gather_up.5.rest_2_ = bf16[1024,1024]{1,0:T(8,128)(2,1)} custom-call(f32[256,1024]{1,0:T(8,128)} %copy-done.22, bf16[256,1024]{1,0:T(8,128)(2,1)} %copy-done.31, bf16[256,1024]{1,0:T(8,128)(2,1)} %collective-permute-done.23.rest_1_, bf16[1024,1024]{1,0:T(8,128)(2,1)} %gather_up.4.rest_2_), custom_call_target="tpu_custom_call", output_to_operand_aliasing={{}: (3, {})} | custom-call | flops 1 | bytes 1 | tf_op jit(solution)/shard_map/f1/gather_up/pallas_call | solution.py:141
  176.7 2.3 %gather_up.6.rest_2_ = bf16[1024,1024]{1,0:T(8,128)(2,1)} custom-call(f32[256,1024]{1,0:T(8,128)} %copy-done.21, bf16[256,1024]{1,0:T(8,128)(2,1)} %collective-permute-done.19.rest_0_, bf16[256,1024]{1,0:T(8,128)(2,1)} %collective-permute-done.20.rest_1_, bf16[1024,1024]{1,0:T(8,128)(2,1)} %gather_up.5.rest_2_), custom_call_target="tpu_custom_call", output_to_operand_aliasing={{}: (3, {})} | custom-call | flops 1 | bytes 1 | tf_op jit(solution)/shard_map/f2/gather_up/pallas_call | solution.py:141
  179.0 8.9 %collective-permute-done.15.rest_1_ = bf16[256,1024]{1,0:T(8,128)(2,1)} collective-permute-done((bf16[256,1024]{1,0:T(8,128)(2,1)S(1)}, bf16[256,1024]{1,0:T(8,128)(2,1)}, u32[]{:S(2)}, u32[]{:S(2)}) %collective-permute-start.15) | collective-permute-done | bytes 524320 | tf_op jit(solution)/shard_map/t32/ppermute | solution.py:337
  188.0 2.4 %gather_up.7 = bf16[1024,1024]{1,0:T(8,128)(2,1)} custom-call(f32[256,1024]{1,0:T(8,128)} %copy-done.20, bf16[256,1024]{1,0:T(8,128)(2,1)} %collective-permute-done.14.rest_0_, bf16[256,1024]{1,0:T(8,128)(2,1)} %collective-permute-done.15.rest_1_, bf16[1024,1024]{1,0:T(8,128)(2,1)} %gather_up.6.rest_2_), custom_call_target="tpu_custom_call", output_to_operand_aliasing={{}: (3, {})} | custom-call | flops 1 | bytes 1 | tf_op jit(solution)/shard_map/f3/gather_up/pallas_call | solution.py:141
  (124 shorter events, 32.8 us)
Async XLA Ops:
  0.0 40.8 %collective-permute-start.7 = (bf16[1024,8192]{1,0:T(8,128)(2,1)}, bf16[1024,8192]{1,0:T(8,128)(2,1)}, u32[]{:S(2)}, u32[]{:S(2)}) collective-permute-start(bf16[1024,8192]{1,0:T(8,128)(2,1)} %w_ref.23), channel_id=1, source_target_pairs={{0,1},{1,0},{2,3},{3,2},{4,5},{5,4},{6,7},{7,6},{8,9},{9,8},{10,11... | collective-permute-start | bytes 50331656 | tf_op jit(solution)/shard_map/ppermute | solution.py:301
  1.8 18.7 %collective-permute-start.3 = (bf16[128,1024]{1,0:T(8,128)(2,1)}, bf16[128,1024]{1,0:T(8,128)(2,1)S(1)}, u32[]{:S(2)}, u32[]{:S(2)}) collective-permute-start(bf16[128,1024]{1,0:T(8,128)(2,1)} %constant_dynamic-slice_fusion), channel_id=1, source_target_pairs={{0,8},{8,0},{16,24},{24,16},{1,9},{9,1},{17,25},{25,17},{2,10},{10... | collective-permute-start | bytes 786440 | tf_op jit(solution)/shard_map/ppermute | solution.py:297
  3.3 9.4 %collective-permute-start.4 = (bf16[128,1024]{1,0:T(8,128)(2,1)}, bf16[128,1024]{1,0:T(8,128)(2,1)S(1)}, u32[]{:S(2)}, u32[]{:S(2)}) collective-permute-start(bf16[128,1024]{1,0:T(8,128)(2,1)} %constant_dynamic-slice_fusion), channel_id=1, source_target_pairs={{0,16},{8,24},{16,0},{24,8},{1,17},{9,25},{17,1},{25,9},{2,18},{10... | collective-permute-start | bytes 786440 | tf_op jit(solution)/shard_map/ppermute | solution.py:296
  4.6 12.2 %collective-permute-start = (bf16[128,1024]{1,0:T(8,128)(2,1)}, bf16[128,1024]{1,0:T(8,128)(2,1)S(1)}, u32[]{:S(2)}, u32[]{:S(2)}) collective-permute-start(bf16[128,1024]{1,0:T(8,128)(2,1)} %constant_dynamic-slice_fusion.1), channel_id=1, source_target_pairs={{0,8},{8,0},{16,24},{24,16},{1,9},{9,1},{17,25},{25,17},{2,10},{10... | collective-permute-start | bytes 786440 | tf_op jit(solution)/shard_map/ppermute | solution.py:295
  5.1 15.5 %collective-permute-start.1 = (bf16[128,1024]{1,0:T(8,128)(2,1)}, bf16[128,1024]{1,0:T(8,128)(2,1)S(1)}, u32[]{:S(2)}, u32[]{:S(2)}) collective-permute-start(bf16[128,1024]{1,0:T(8,128)(2,1)} %constant_dynamic-slice_fusion.1), channel_id=1, source_target_pairs={{0,16},{8,24},{16,0},{24,8},{1,17},{9,25},{17,1},{25,9},{2,18},{10... | collective-permute-start | bytes 786440 | tf_op jit(solution)/shard_map/ppermute | solution.py:298
  12.7 9.1 %collective-permute-start.5 = (bf16[128,1024]{1,0:T(8,128)(2,1)S(1)}, bf16[128,1024]{1,0:T(8,128)(2,1)S(1)}, u32[]{:S(2)}, u32[]{:S(2)}) collective-permute-start(bf16[128,1024]{1,0:T(8,128)(2,1)S(1)} %collective-permute-done.4), channel_id=1, source_target_pairs={{0,8},{8,0},{16,24},{24,16},{1,9},{9,1},{17,25},{25,17},{2,10},{10... | collective-permute-start | bytes 786440 | tf_op jit(solution)/shard_map/ppermute | solution.py:300
  16.8 7.3 %collective-permute-start.2 = (bf16[128,1024]{1,0:T(8,128)(2,1)S(1)}, bf16[128,1024]{1,0:T(8,128)(2,1)}, u32[]{:S(2)}, u32[]{:S(2)}) collective-permute-start(bf16[128,1024]{1,0:T(8,128)(2,1)S(1)} %collective-permute-done), channel_id=1, source_target_pairs={{0,16},{8,24},{16,0},{24,8},{1,17},{9,25},{17,1},{25,9},{2,18},{10... | collective-permute-start | bytes 786440 | tf_op jit(solution)/shard_map/ppermute | solution.py:299
  31.6 44.9 %copy-start.2 = (bf16[256,1024]{1,0:T(8,128)(2,1)}, bf16[256,1024]{1,0:T(8,128)(2,1)S(1)}, u32[]{:S(2)}) copy-start(bf16[256,1024]{1,0:T(8,128)(2,1)S(1)} %attend.3.refs_0_.own_ref) | copy-start | bytes 1572868
  31.6 9.2 %collective-permute-start.8 = (bf16[256,1024]{1,0:T(8,128)(2,1)S(1)}, bf16[256,1024]{1,0:T(8,128)(2,1)S(1)}, u32[]{:S(2)}, u32[]{:S(2)}) collective-permute-start(bf16[256,1024]{1,0:T(8,128)(2,1)S(1)} %attend.3.refs_0_.own_ref), channel_id=1, source_target_pairs={{0,1},{1,0},{2,3},{3,2},{4,5},{5,4},{6,7},{7,6},{8,9},{9,8},{10,11... | collective-permute-start | bytes 1572872 | tf_op jit(solution)/shard_map/a0/ppermute | solution.py:317
  40.1 30.9 %copy-start.4 = (bf16[256,1024]{1,0:T(8,128)(2,1)}, bf16[256,1024]{1,0:T(8,128)(2,1)S(1)}, u32[]{:S(2)}) copy-start(bf16[256,1024]{1,0:T(8,128)(2,1)S(1)} %attend.4.own_ref.refs_1_) | copy-start | bytes 1572868
  40.1 4.3 %collective-permute-start.6 = (bf16[256,1024]{1,0:T(8,128)(2,1)S(1)}, bf16[256,1024]{1,0:T(8,128)(2,1)S(1)}, u32[]{:S(2)}, u32[]{:S(2)}) collective-permute-start(bf16[256,1024]{1,0:T(8,128)(2,1)S(1)} %attend.4.own_ref.refs_1_), channel_id=1, source_target_pairs={{0,1},{1,0},{2,3},{3,2},{4,5},{5,4},{6,7},{7,6},{8,9},{9,8},{10,11... | collective-permute-start | bytes 1572872 | tf_op jit(solution)/shard_map/a1/ppermute | solution.py:317
  40.8 35.7 %copy-start.6 = (bf16[256,1024]{1,0:T(8,128)(2,1)}, bf16[256,1024]{1,0:T(8,128)(2,1)S(1)}, u32[]{:S(2)}) copy-start(bf16[256,1024]{1,0:T(8,128)(2,1)S(1)} %collective-permute-done.8.refs_4_.other_ref) | copy-start | bytes 1572868
  43.7 14.8 %collective-permute-start.16 = (bf16[256,2048]{1,0:T(8,128)(2,1)S(1)}, bf16[256,2048]{1,0:T(8,128)(2,1)S(1)}, u32[]{:S(2)}, u32[]{:S(2)}) collective-permute-start(bf16[256,2048]{1,0:T(8,128)(2,1)S(1)} %unit.16), channel_id=1, source_target_pairs={{0,2},{7,5},{8,10},{15,13},{16,18},{23,21},{24,26},{31,29}} | collective-permute-start | bytes 3145736 | tf_op jit(solution)/shard_map/t00/ppermute | solution.py:337
  47.4 18.1 %collective-permute-start.11 = (bf16[256,2048]{1,0:T(8,128)(2,1)S(1)}, bf16[256,2048]{1,0:T(8,128)(2,1)S(1)}, u32[]{:S(2)}, u32[]{:S(2)}) collective-permute-start(bf16[256,2048]{1,0:T(8,128)(2,1)S(1)} %unit.12), channel_id=1, source_target_pairs={{0,2},{7,5},{8,10},{15,13},{16,18},{23,21},{24,26},{31,29}} | collective-permute-start | bytes 3145736 | tf_op jit(solution)/shard_map/t10/ppermute | solution.py:337
  57.2 2.8 %collective-permute-start.9 = (bf16[256,1024]{1,0:T(8,128)(2,1)S(1)}, bf16[256,1024]{1,0:T(8,128)(2,1)S(1)}, u32[]{:S(2)}, u32[]{:S(2)}) collective-permute-start(bf16[256,1024]{1,0:T(8,128)(2,1)S(1)} %get-tuple-element.26.refs_2_.own_ref), channel_id=1, source_target_pairs={{0,1},{1,0},{2,3},{3,2},{4,5},{5,4},{6,7},{7,6},{8,9},{9,8},{10,11... | collective-permute-start | bytes 1572872 | tf_op jit(solution)/shard_map/a2/ppermute | solution.py:317
  58.4 7.1 %collective-permute-start.10 = (bf16[256,1024]{1,0:T(8,128)(2,1)S(1)}, bf16[256,1024]{1,0:T(8,128)(2,1)S(1)}, u32[]{:S(2)}, u32[]{:S(2)}) collective-permute-start(bf16[256,1024]{1,0:T(8,128)(2,1)S(1)} %get-tuple-element.27.refs_3_.own_ref), channel_id=1, source_target_pairs={{0,1},{1,0},{2,3},{3,2},{4,5},{5,4},{6,7},{7,6},{8,9},{9,8},{10,11... | collective-permute-start | bytes 1572872 | tf_op jit(solution)/shard_map/a2/ppermute | solution.py:317
  63.8 18.0 %collective-permute-start.17 = (bf16[256,2048]{1,0:T(8,128)(2,1)}, bf16[256,2048]{1,0:T(8,128)(2,1)}, u32[]{:S(2)}, u32[]{:S(2)}) collective-permute-start(bf16[256,2048]{1,0:T(8,128)(2,1)} %unit.17), channel_id=1, source_target_pairs={{0,2},{7,5},{8,10},{15,13},{16,18},{23,21},{24,26},{31,29}} | collective-permute-start | bytes 3145736 | tf_op jit(solution)/shard_map/t20/ppermute | solution.py:337
  69.3 17.7 %collective-permute-start.12 = (bf16[256,2048]{1,0:T(8,128)(2,1)}, bf16[256,2048]{1,0:T(8,128)(2,1)}, u32[]{:S(2)}, u32[]{:S(2)}) collective-permute-start(bf16[256,2048]{1,0:T(8,128)(2,1)} %unit.13), channel_id=1, source_target_pairs={{0,2},{7,5},{8,10},{15,13},{16,18},{23,21},{24,26},{31,29}} | collective-permute-start | bytes 3145736 | tf_op jit(solution)/shard_map/t30/ppermute | solution.py:337
  74.8 28.2 %collective-permute-start.21 = (bf16[256,2048]{1,0:T(8,128)(2,1)}, bf16[256,2048]{1,0:T(8,128)(2,1)}, u32[]{:S(2)}, u32[]{:S(2)}) collective-permute-start(bf16[256,2048]{1,0:T(8,128)(2,1)} %unit.20), channel_id=1, source_target_pairs={{0,2},{7,5},{2,4},{5,3},{8,10},{15,13},{10,12},{13,11},{16,18},{23... | collective-permute-start | bytes 3145736 | tf_op jit(solution)/shard_map/t11/ppermute | solution.py:337
  80.3 35.6 %collective-permute-start.24 = (bf16[256,2048]{1,0:T(8,128)(2,1)}, bf16[256,2048]{1,0:T(8,128)(2,1)}, u32[]{:S(2)}, u32[]{:S(2)}) collective-permute-start(bf16[256,2048]{1,0:T(8,128)(2,1)} %unit.22), channel_id=1, source_target_pairs={{0,2},{7,5},{2,4},{5,3},{8,10},{15,13},{10,12},{13,11},{16,18},{23... | collective-permute-start | bytes 3145736 | tf_op jit(solution)/shard_map/t01/ppermute | solution.py:337
  85.7 59.4 %collective-permute-start.18 = (bf16[256,2048]{1,0:T(8,128)(2,1)}, bf16[256,2048]{1,0:T(8,128)(2,1)}, u32[]{:S(2)}, u32[]{:S(2)}) collective-permute-start(bf16[256,2048]{1,0:T(8,128)(2,1)} %unit.18), channel_id=1, source_target_pairs={{0,2},{7,5},{2,4},{5,3},{8,10},{15,13},{10,12},{13,11},{16,18},{23... | collective-permute-start | bytes 3145736 | tf_op jit(solution)/shard_map/t21/ppermute | solution.py:337
  90.1 62.7 %collective-permute-start.13 = (bf16[256,2048]{1,0:T(8,128)(2,1)S(1)}, bf16[256,2048]{1,0:T(8,128)(2,1)}, u32[]{:S(2)}, u32[]{:S(2)}) collective-permute-start(bf16[256,2048]{1,0:T(8,128)(2,1)S(1)} %unit.14), channel_id=1, source_target_pairs={{0,2},{7,5},{2,4},{5,3},{8,10},{15,13},{10,12},{13,11},{16,18},{23... | collective-permute-start | bytes 3145736 | tf_op jit(solution)/shard_map/t31/ppermute | solution.py:337
  108.7 38.5 %copy-start.13 = (bf16[256,1024]{1,0:T(8,128)(2,1)S(1)}, bf16[256,1024]{1,0:T(8,128)(2,1)}, u32[]{:S(2)}) copy-start(bf16[256,1024]{1,0:T(8,128)(2,1)} %copy-done.12) | copy-start | bytes 1572868
  108.7 38.5 %copy-start.19 = (bf16[256,1024]{1,0:T(8,128)(2,1)S(1)}, bf16[256,1024]{1,0:T(8,128)(2,1)}, u32[]{:S(2)}) copy-start(bf16[256,1024]{1,0:T(8,128)(2,1)} %copy-done.17) | copy-start | bytes 1572868
  108.7 51.6 %collective-permute-start.22 = (bf16[256,1024]{1,0:T(8,128)(2,1)S(1)}, bf16[256,1024]{1,0:T(8,128)(2,1)S(1)}, u32[]{:S(2)}, u32[]{:S(2)}) collective-permute-start(bf16[256,1024]{1,0:T(8,128)(2,1)S(1)} %get-tuple-element.37), channel_id=1, source_target_pairs={{0,2},{7,5},{2,4},{5,3},{4,6},{3,1},{8,10},{15,13},{10,12},{13,11}... | collective-permute-start | bytes 1572872 | tf_op jit(solution)/shard_map/t12/ppermute | solution.py:337
  121.5 42.6 %collective-permute-start.25 = (bf16[256,1024]{1,0:T(8,128)(2,1)S(1)}, bf16[256,1024]{1,0:T(8,128)(2,1)S(1)}, u32[]{:S(2)}, u32[]{:S(2)}) collective-permute-start(bf16[256,1024]{1,0:T(8,128)(2,1)S(1)} %get-tuple-element.41), channel_id=1, source_target_pairs={{0,2},{7,5},{2,4},{5,3},{4,6},{3,1},{8,10},{15,13},{10,12},{13,11}... | collective-permute-start | bytes 1572872 | tf_op jit(solution)/shard_map/t02/ppermute | solution.py:337
  123.5 42.6 %collective-permute-start.26 = (bf16[256,1024]{1,0:T(8,128)(2,1)S(1)}, bf16[256,1024]{1,0:T(8,128)(2,1)S(1)}, u32[]{:S(2)}, u32[]{:S(2)}) collective-permute-start(bf16[256,1024]{1,0:T(8,128)(2,1)S(1)} %get-tuple-element.42), channel_id=1, source_target_pairs={{0,3},{7,4},{2,5},{5,2},{4,7},{3,0},{8,11},{15,12},{10,13},{13,10}... | collective-permute-start | bytes 1572872 | tf_op jit(solution)/shard_map/t02/ppermute | solution.py:337
  145.2 28.3 %collective-permute-start.23 = (bf16[256,1024]{1,0:T(8,128)(2,1)S(1)}, bf16[256,1024]{1,0:T(8,128)(2,1)}, u32[]{:S(2)}, u32[]{:S(2)}) collective-permute-start(bf16[256,1024]{1,0:T(8,128)(2,1)S(1)} %get-tuple-element.38), channel_id=1, source_target_pairs={{0,3},{7,4},{2,5},{5,2},{4,7},{3,0},{8,11},{15,12},{10,13},{13,10}... | collective-permute-start | bytes 1572872 | tf_op jit(solution)/shard_map/t12/ppermute | solution.py:337
  152.8 23.0 %collective-permute-start.19 = (bf16[256,1024]{1,0:T(8,128)(2,1)S(1)}, bf16[256,1024]{1,0:T(8,128)(2,1)}, u32[]{:S(2)}, u32[]{:S(2)}) collective-permute-start(bf16[256,1024]{1,0:T(8,128)(2,1)S(1)} %get-tuple-element.34), channel_id=1, source_target_pairs={{0,2},{7,5},{2,4},{5,3},{4,6},{3,1},{8,10},{15,13},{10,12},{13,11}... | collective-permute-start | bytes 1572872 | tf_op jit(solution)/shard_map/t22/ppermute | solution.py:337
  160.3 16.4 %collective-permute-start.20 = (bf16[256,1024]{1,0:T(8,128)(2,1)S(1)}, bf16[256,1024]{1,0:T(8,128)(2,1)}, u32[]{:S(2)}, u32[]{:S(2)}) collective-permute-start(bf16[256,1024]{1,0:T(8,128)(2,1)S(1)} %get-tuple-element.35), channel_id=1, source_target_pairs={{0,3},{7,4},{2,5},{5,2},{4,7},{3,0},{8,11},{15,12},{10,13},{13,10}... | collective-permute-start | bytes 1572872 | tf_op jit(solution)/shard_map/t22/ppermute | solution.py:337
  164.1 14.9 %collective-permute-start.14 = (bf16[256,1024]{1,0:T(8,128)(2,1)S(1)}, bf16[256,1024]{1,0:T(8,128)(2,1)}, u32[]{:S(2)}, u32[]{:S(2)}) collective-permute-start(bf16[256,1024]{1,0:T(8,128)(2,1)S(1)} %get-tuple-element.30), channel_id=1, source_target_pairs={{0,2},{7,5},{2,4},{5,3},{4,6},{3,1},{8,10},{15,13},{10,12},{13,11}... | collective-permute-start | bytes 1572872 | tf_op jit(solution)/shard_map/t32/ppermute | solution.py:337
  166.9 21.1 %collective-permute-start.15 = (bf16[256,1024]{1,0:T(8,128)(2,1)S(1)}, bf16[256,1024]{1,0:T(8,128)(2,1)}, u32[]{:S(2)}, u32[]{:S(2)}) collective-permute-start(bf16[256,1024]{1,0:T(8,128)(2,1)S(1)} %get-tuple-element.31), channel_id=1, source_target_pairs={{0,3},{7,4},{2,5},{5,2},{4,7},{3,0},{8,11},{15,12},{10,13},{13,10}... | collective-permute-start | bytes 1572872 | tf_op jit(solution)/shard_map/t32/ppermute | solution.py:337
  (29 other events, 238.2 us)

commit v3 on v2

--- a/solution.py
+++ b/solution.py
@@ -353,8 +353,7 @@
     attention, tick, own_part, finish = [
         named(f, n) for f, n in ((attention, "a"), (tick, "t"), (own_part, "o"), (finish, "f"))
     ]
-    attention(0)
-    attention(1, mine[0])
+    attention(0, count=2)
     tick(0, 0)
     tick(1, 0)
     attention(2, mine[1], sent[1, 0][0], count=2)

time: 190 us -> 190 us (level); the launches traced: 190 us -> 188 us
  Pallas kernels: 93.2 us -> 89.2 us
    pallas_call x3 -> x2, Pallas kernels: 24.9 us -> 20.9 us  [attend(): pl.pallas_call(functools.partial(attend_kernel, row_tile, block_len, (til...]
  transfers between devices with their start and end apart: 27 -> 27, of which waited for: 7 -> 8; matrix products, arithmetic and copies ran while one was open for 4% -> 4% of each run, Pallas kernels for 48% -> 46%
where the time goes in v3:
time: 190 us; the launch traced here: 188 us
  Pallas kernels  89.2 us (47%)
  starting transfers between devices  62.2 us (33%)
  waiting for transfers between devices  24.1 us (13%)
  local copies, waits for them, and re-layouts  8.88 us (5%)
  other arithmetic  2.8 us (1%)
    ppermute x16, starting transfers between devices, tick(): lax.ppermute(sent[k, s][cross], 'head', pairs)  55.1 us
    pallas_call x12, Pallas kernels, unit(): pl.pallas_call(functools.partial(unit_kernel, len(adds), n_out), out_shap...  50.4 us
    pallas_call x2, Pallas kernels, attend(): pl.pallas_call(functools.partial(attend_kernel, row_tile, block_len, (til...  20.9 us
    ppermute x16, waiting for transfers between devices, tick(): lax.ppermute(sent[k, s][cross], 'head', pairs)  9.92 us
    pallas_call x4, Pallas kernels, gather_up(): pl.pallas_call(gather_kernel, out_shape=jax.ShapeDtypeStruct((total_rows,...  9.34 us
    pallas_call x1, Pallas kernels, own_product(): pl.pallas_call(functools.partial(own_kernel, n), out_shape=[jax.ShapeDtyp...  8.5 us
    ppermute x1, waiting for transfers between devices, line(): values_2 = lax.ppermute(values, 'ctx', along[1])  4.35 us
    unnamed x68, local copies, waits for them, and re-layouts  3.85 us
  transfers between devices with their start and end apart: 27, of which 8 were waited for; matrix products, arithmetic and copies ran while one was open for 4% of the time, Pallas kernels for 46%

profile of v3, /device:TPU:20, one launch (start us, length us, event | category | flops | bytes accessed | tf_op | source)
XLA Modules:
  0.0 187.8 jit_solution(15240233424127301452)
XLA Ops:
  0.0 1.8 constant_dynamic-slice_fusion
  8.4 4.3 %collective-permute-done.4 = bf16[128,1024]{1,0:T(8,128)(2,1)S(1)} collective-permute-done((bf16[128,1024]{1,0:T(8,128)(2,1)}, bf16[128,1024]{1,0:T(8,128)(2,1)S(1)}, u32[]{:S(2)}, u32[]{:S(2)}) %collective-permute-start.4) | collective-permute-done | bytes 262176 | tf_op jit(solution)/shard_map/ppermute | solution.py:296
  13.2 3.5 %collective-permute-done = bf16[128,1024]{1,0:T(8,128)(2,1)S(1)} collective-permute-done((bf16[128,1024]{1,0:T(8,128)(2,1)}, bf16[128,1024]{1,0:T(8,128)(2,1)S(1)}, u32[]{:S(2)}, u32[]{:S(2)}) %collective-permute-start) | collective-permute-done | bytes 262176 | tf_op jit(solution)/shard_map/ppermute | solution.py:295
  21.8 2.2 %collective-permute-done.2 = bf16[128,1024]{1,0:T(8,128)(2,1)} collective-permute-done((bf16[128,1024]{1,0:T(8,128)(2,1)S(1)}, bf16[128,1024]{1,0:T(8,128)(2,1)}, u32[]{:S(2)}, u32[]{:S(2)}) %collective-permute-start.2) | collective-permute-done | bytes 262176 | tf_op jit(solution)/shard_map/ppermute | solution.py:299
  24.1 11.0 %attend.2 = (bf16[256,1024]{1,0:T(8,128)(2,1)S(1)}, bf16[256,1024]{1,0:T(8,128)(2,1)S(1)}) custom-call(s32[22]{0:T(128)S(1)} %concatenate.3.scal, bf16[1024,1024]{1,0:T(8,128)(2,1)} %q_ref.3, bf16[1,128,1024]{2,1,0:T(8,128)(2,1)} %fusion.2.rest_0_, bf16[1,128,1024]{2,1,0:T(8,128)(2,1)} %bitcast.26, bf16[1,128,1024]{2,1,0:T(8,128)(2,1)} %bitcast.28, ...), custom_call_target="tpu_custom_call" | custom-call | flops 1 | bytes 1 | tf_op jit(solution)/shard_map/a0/attend/pallas_call | solution.py:100
  37.1 2.9 %unit.16 = bf16[256,2048]{1,0:T(8,128)(2,1)S(1)} custom-call(s32[3]{0:T(128)S(1)} %add_add_fusion.scal, bf16[256,1024]{1,0:T(8,128)(2,1)S(1)} %get-tuple-element.25.refs_0_.own_ref, bf16[256,1024]{1,0:T(8,128)(2,1)S(1)} %collective-permute-done.8.refs_4_.other_ref, bf16[1024,8192]{1,0:T(8,128)(2,1)} %w_ref.23, ...), custom_call_target="tpu_custom_call" | custom-call | flops 1 | bytes 1 | tf_op jit(solution)/shard_map/t00/unit/pallas_call | solution.py:189
  40.8 2.9 %unit.12 = bf16[256,2048]{1,0:T(8,128)(2,1)S(1)} custom-call(s32[3]{0:T(128)S(1)} %add_add_fusion.scal, bf16[256,1024]{1,0:T(8,128)(2,1)S(1)} %get-tuple-element.26.own_ref.refs_1_, bf16[256,1024]{1,0:T(8,128)(2,1)S(1)} %collective-permute-done.6.other_ref.refs_5_, bf16[1024,8192]{1,0:T(8,128)(2,1)} %w_ref.23, ...), custom_call_target="tpu_custom_call" | custom-call | flops 1 | bytes 1 | tf_op jit(solution)/shard_map/t10/unit/pallas_call | solution.py:189
  44.4 10.0 %attend.3 = (bf16[256,1024]{1,0:T(8,128)(2,1)S(1)}, bf16[256,1024]{1,0:T(8,128)(2,1)S(1)}) custom-call(s32[22]{0:T(128)S(1)} %concatenate.3.scal, bf16[1024,1024]{1,0:T(8,128)(2,1)} %q_ref.3, bf16[1,128,1024]{2,1,0:T(8,128)(2,1)} %fusion.2.rest_0_, bf16[1,128,1024]{2,1,0:T(8,128)(2,1)} %bitcast.27, bf16[1,128,1024]{2,1,0:T(8,128)(2,1)} %bitcast.29, ...), custom_call_target="tpu_custom_call" | custom-call | flops 1 | bytes 1 | tf_op jit(solution)/shard_map/a2/attend/pallas_call | solution.py:100
  57.3 3.8 %unit.17 = bf16[256,2048]{1,0:T(8,128)(2,1)} custom-call(s32[3]{0:T(128)S(1)} %add_add_fusion.scal, bf16[256,1024]{1,0:T(8,128)(2,1)S(1)} %get-tuple-element.28.refs_2_.own_ref, bf16[256,1024]{1,0:T(8,128)(2,1)S(1)} %collective-permute-done.9.refs_6_.other_ref, bf16[1024,8192]{1,0:T(8,128)(2,1)} %w_ref.23, ...), custom_call_target="tpu_custom_call" | custom-call | flops 1 | bytes 1 | tf_op jit(solution)/shard_map/t20/unit/pallas_call | solution.py:189
  62.9 3.8 %unit.13 = bf16[256,2048]{1,0:T(8,128)(2,1)} custom-call(s32[3]{0:T(128)S(1)} %add_add_fusion.scal, bf16[256,1024]{1,0:T(8,128)(2,1)S(1)} %get-tuple-element.29.refs_3_.own_ref, bf16[256,1024]{1,0:T(8,128)(2,1)S(1)} %collective-permute-done.10.refs_7_.other_ref, bf16[1024,8192]{1,0:T(8,128)(2,1)} %w_ref.23, ...), custom_call_target="tpu_custom_call" | custom-call | flops 1 | bytes 1 | tf_op jit(solution)/shard_map/t30/unit/pallas_call | solution.py:189
  68.4 3.9 %unit.20 = bf16[256,2048]{1,0:T(8,128)(2,1)} custom-call(s32[3]{0:T(128)S(1)} %add_add_fusion.2.scal, bf16[256,1024]{1,0:T(8,128)(2,1)S(1)} %get-tuple-element.26.own_ref.refs_1_, bf16[256,1024]{1,0:T(8,128)(2,1)S(1)} %collective-permute-done.6.other_ref.refs_5_, bf16[1024,8192]{1,0:T(8,128)(2,1)} %w_ref.23, ...), custom_call_target="tpu_custom_call" | custom-call | flops 1 | bytes 1 | tf_op jit(solution)/shard_map/t11/unit/pallas_call | solution.py:189
  73.7 3.9 %unit.22 = bf16[256,2048]{1,0:T(8,128)(2,1)} custom-call(s32[3]{0:T(128)S(1)} %add_add_fusion.2.scal, bf16[256,1024]{1,0:T(8,128)(2,1)S(1)} %get-tuple-element.25.refs_0_.own_ref, bf16[256,1024]{1,0:T(8,128)(2,1)S(1)} %collective-permute-done.8.refs_4_.other_ref, bf16[1024,8192]{1,0:T(8,128)(2,1)} %w_ref.23, ...), custom_call_target="tpu_custom_call" | custom-call | flops 1 | bytes 1 | tf_op jit(solution)/shard_map/t01/unit/pallas_call | solution.py:189
  79.0 3.9 %unit.18 = bf16[256,2048]{1,0:T(8,128)(2,1)} custom-call(s32[3]{0:T(128)S(1)} %add_add_fusion.2.scal, bf16[256,1024]{1,0:T(8,128)(2,1)S(1)} %get-tuple-element.28.refs_2_.own_ref, bf16[256,1024]{1,0:T(8,128)(2,1)S(1)} %copy-done.18, bf16[1024,8192]{1,0:T(8,128)(2,1)} %w_ref.23, bf16[1024,8192]{1,0:T(8,128)(2,1)} %collective-permute-done.7.wp_ref.refs_9_, ...), custom_call_target="tpu_custom_call" | custom-call | flops 1 | bytes 1 | tf_op jit(solution)/shard_map/t21/unit/pallas_call | solution.py:189
  84.4 3.0 %unit.14 = bf16[256,2048]{1,0:T(8,128)(2,1)S(1)} custom-call(s32[3]{0:T(128)S(1)} %add_add_fusion.2.scal, bf16[256,1024]{1,0:T(8,128)(2,1)S(1)} %get-tuple-element.29.refs_3_.own_ref, bf16[256,1024]{1,0:T(8,128)(2,1)S(1)} %copy-done.15, bf16[1024,8192]{1,0:T(8,128)(2,1)} %w_ref.23, bf16[1024,8192]{1,0:T(8,128)(2,1)} %collective-permute-done.7.wp_ref.refs_9_, ...), custom_call_target="tpu_custom_call" | custom-call | flops 1 | bytes 1 | tf_op jit(solution)/shard_map/t31/unit/pallas_call | solution.py:189
  89.0 8.5 %own_product.1 = (f32[256,1024]{1,0:T(8,128)S(1)}, f32[256,1024]{1,0:T(8,128)S(1)}, f32[256,1024]{1,0:T(8,128)S(1)}, f32[256,1024]{1,0:T(8,128)S(1)}) custom-call(s32[3]{0:T(128)S(1)} %pad_add_fusion.scal, bf16[256,1024]{1,0:T(8,128)(2,1)} %copy-done.2, bf16[256,1024]{1,0:T(8,128)(2,1)} %copy-done.6, bf16[256,1024]{1,0:T(8,128)(2,1)} %copy-done.12, ...), custom_call_target="tpu_custom_call" | custom-call | flops 1 | bytes 1 | tf_op jit(solution)/shard_map/o/own_product/pallas_call | solution.py:218
  100.5 5.6 %unit.21 = (bf16[256,1024]{1,0:T(8,128)(2,1)S(1)}, bf16[256,1024]{1,0:T(8,128)(2,1)S(1)}) custom-call(s32[3]{0:T(128)S(1)} %add_add_fusion.1.scal, bf16[256,1024]{1,0:T(8,128)(2,1)S(1)} %copy-done.7, bf16[256,1024]{1,0:T(8,128)(2,1)S(1)} %copy-done.9, bf16[1024,8192]{1,0:T(8,128)(2,1)} %w_ref.23, bf16[1024,8192]{1,0:T(8,128)(2,1)} %collective-permute-done.7.wp_ref.refs_9_, ...), custom_call_target="tpu_custom_call" | custom-call | flops 1 | bytes 1 | tf_op jit(solution)/shard_map/t12/unit/pallas_call | solution.py:189
  106.1 7.2 %collective-permute-start.22 = (bf16[256,1024]{1,0:T(8,128)(2,1)S(1)}, bf16[256,1024]{1,0:T(8,128)(2,1)S(1)}, u32[]{:S(2)}, u32[]{:S(2)}) collective-permute-start(bf16[256,1024]{1,0:T(8,128)(2,1)S(1)} %get-tuple-element.39), channel_id=1, source_target_pairs={{0,2},{7,5},{2,4},{5,3},{4,6},{3,1},{8,10},{15,13},{10,12},{13,11}... | collective-permute-start | bytes 1572872 | tf_op jit(solution)/shard_map/t12/ppermute | solution.py:337
  113.3 5.5 %unit.23 = (bf16[256,1024]{1,0:T(8,128)(2,1)S(1)}, bf16[256,1024]{1,0:T(8,128)(2,1)S(1)}) custom-call(s32[3]{0:T(128)S(1)} %add_add_fusion.1.scal, bf16[256,1024]{1,0:T(8,128)(2,1)S(1)} %copy-done.3, bf16[256,1024]{1,0:T(8,128)(2,1)S(1)} %copy-done.5, bf16[1024,8192]{1,0:T(8,128)(2,1)} %w_ref.23, bf16[1024,8192]{1,0:T(8,128)(2,1)} %collective-permute-done.7.wp_ref.refs_9_, ...), custom_call_target="tpu_custom_call" | custom-call | flops 1 | bytes 1 | tf_op jit(solution)/shard_map/t02/unit/pallas_call | solution.py:189
  118.9 1.9 %collective-permute-start.25 = (bf16[256,1024]{1,0:T(8,128)(2,1)S(1)}, bf16[256,1024]{1,0:T(8,128)(2,1)S(1)}, u32[]{:S(2)}, u32[]{:S(2)}) collective-permute-start(bf16[256,1024]{1,0:T(8,128)(2,1)S(1)} %get-tuple-element.43), channel_id=1, source_target_pairs={{0,2},{7,5},{2,4},{5,3},{4,6},{3,1},{8,10},{15,13},{10,12},{13,11}... | collective-permute-start | bytes 1572872 | tf_op jit(solution)/shard_map/t02/ppermute | solution.py:337
  120.8 21.7 %collective-permute-start.26 = (bf16[256,1024]{1,0:T(8,128)(2,1)S(1)}, bf16[256,1024]{1,0:T(8,128)(2,1)S(1)}, u32[]{:S(2)}, u32[]{:S(2)}) collective-permute-start(bf16[256,1024]{1,0:T(8,128)(2,1)S(1)} %get-tuple-element.44), channel_id=1, source_target_pairs={{0,3},{7,4},{2,5},{5,2},{4,7},{3,0},{8,11},{15,12},{10,13},{13,10}... | collective-permute-start | bytes 1572872 | tf_op jit(solution)/shard_map/t02/ppermute | solution.py:337
  142.6 2.1 %collective-permute-start.23 = (bf16[256,1024]{1,0:T(8,128)(2,1)S(1)}, bf16[256,1024]{1,0:T(8,128)(2,1)}, u32[]{:S(2)}, u32[]{:S(2)}) collective-permute-start(bf16[256,1024]{1,0:T(8,128)(2,1)S(1)} %get-tuple-element.40), channel_id=1, source_target_pairs={{0,3},{7,4},{2,5},{5,2},{4,7},{3,0},{8,11},{15,12},{10,13},{13,10}... | collective-permute-start | bytes 1572872 | tf_op jit(solution)/shard_map/t12/ppermute | solution.py:337
  144.6 5.5 %unit.19 = (bf16[256,1024]{1,0:T(8,128)(2,1)S(1)}, bf16[256,1024]{1,0:T(8,128)(2,1)S(1)}) custom-call(s32[3]{0:T(128)S(1)} %add_add_fusion.1.scal, bf16[256,1024]{1,0:T(8,128)(2,1)S(1)} %copy-done.13, bf16[256,1024]{1,0:T(8,128)(2,1)S(1)} %copy-done.19, bf16[1024,8192]{1,0:T(8,128)(2,1)} %w_ref.23, bf16[1024,8192]{1,0:T(8,128)(2,1)} %collective-permute-done.7.wp_ref.refs_9_, ...), custom_call_target="tpu_custom_call" | custom-call | flops 1 | bytes 1 | tf_op jit(solution)/shard_map/t22/unit/pallas_call | solution.py:189
  150.2 1.9 %collective-permute-start.19 = (bf16[256,1024]{1,0:T(8,128)(2,1)S(1)}, bf16[256,1024]{1,0:T(8,128)(2,1)}, u32[]{:S(2)}, u32[]{:S(2)}) collective-permute-start(bf16[256,1024]{1,0:T(8,128)(2,1)S(1)} %get-tuple-element.36), channel_id=1, source_target_pairs={{0,2},{7,5},{2,4},{5,3},{4,6},{3,1},{8,10},{15,13},{10,12},{13,11}... | collective-permute-start | bytes 1572872 | tf_op jit(solution)/shard_map/t22/ppermute | solution.py:337
  152.2 5.5 %unit.15 = (bf16[256,1024]{1,0:T(8,128)(2,1)S(1)}, bf16[256,1024]{1,0:T(8,128)(2,1)S(1)}) custom-call(s32[3]{0:T(128)S(1)} %add_add_fusion.1.scal, bf16[256,1024]{1,0:T(8,128)(2,1)S(1)} %copy-done.11, bf16[256,1024]{1,0:T(8,128)(2,1)S(1)} %copy-done.16, bf16[1024,8192]{1,0:T(8,128)(2,1)} %w_ref.23, bf16[1024,8192]{1,0:T(8,128)(2,1)} %collective-permute-done.7.wp_ref.refs_9_, ...), custom_call_target="tpu_custom_call" | custom-call | flops 1 | bytes 1 | tf_op jit(solution)/shard_map/t32/unit/pallas_call | solution.py:189
  157.7 3.8 %collective-permute-start.20 = (bf16[256,1024]{1,0:T(8,128)(2,1)S(1)}, bf16[256,1024]{1,0:T(8,128)(2,1)}, u32[]{:S(2)}, u32[]{:S(2)}) collective-permute-start(bf16[256,1024]{1,0:T(8,128)(2,1)S(1)} %get-tuple-element.37), channel_id=1, source_target_pairs={{0,3},{7,4},{2,5},{5,2},{4,7},{3,0},{8,11},{15,12},{10,13},{13,10}... | collective-permute-start | bytes 1572872 | tf_op jit(solution)/shard_map/t22/ppermute | solution.py:337
  161.5 1.9 %collective-permute-start.14 = (bf16[256,1024]{1,0:T(8,128)(2,1)S(1)}, bf16[256,1024]{1,0:T(8,128)(2,1)}, u32[]{:S(2)}, u32[]{:S(2)}) collective-permute-start(bf16[256,1024]{1,0:T(8,128)(2,1)S(1)} %get-tuple-element.32), channel_id=1, source_target_pairs={{0,2},{7,5},{2,4},{5,3},{4,6},{3,1},{8,10},{15,13},{10,12},{13,11}... | collective-permute-start | bytes 1572872 | tf_op jit(solution)/shard_map/t32/ppermute | solution.py:337
  164.3 4.3 %collective-permute-start.15 = (bf16[256,1024]{1,0:T(8,128)(2,1)S(1)}, bf16[256,1024]{1,0:T(8,128)(2,1)}, u32[]{:S(2)}, u32[]{:S(2)}) collective-permute-start(bf16[256,1024]{1,0:T(8,128)(2,1)S(1)} %get-tuple-element.33), channel_id=1, source_target_pairs={{0,3},{7,4},{2,5},{5,2},{4,7},{3,0},{8,11},{15,12},{10,13},{13,10}... | collective-permute-start | bytes 1572872 | tf_op jit(solution)/shard_map/t32/ppermute | solution.py:337
  168.5 2.3 %gather_up.4.rest_2_ = bf16[1024,1024]{1,0:T(8,128)(2,1)} custom-call(f32[256,1024]{1,0:T(8,128)} %copy-done.23, bf16[256,1024]{1,0:T(8,128)(2,1)} %copy-done.32, bf16[256,1024]{1,0:T(8,128)(2,1)} %copy-done.33), custom_call_target="tpu_custom_call" | custom-call | flops 1 | bytes 1 | tf_op jit(solution)/shard_map/f0/gather_up/pallas_call | solution.py:141
  170.9 2.3 %gather_up.5.rest_2_ = bf16[1024,1024]{1,0:T(8,128)(2,1)} custom-call(f32[256,1024]{1,0:T(8,128)} %copy-done.22, bf16[256,1024]{1,0:T(8,128)(2,1)} %copy-done.31, bf16[256,1024]{1,0:T(8,128)(2,1)} %collective-permute-done.23.rest_1_, bf16[1024,1024]{1,0:T(8,128)(2,1)} %gather_up.4.rest_2_), custom_call_target="tpu_custom_call", output_to_operand_aliasing={{}: (3, {})} | custom-call | flops 1 | bytes 1 | tf_op jit(solution)/shard_map/f1/gather_up/pallas_call | solution.py:141
  174.1 2.3 %gather_up.6.rest_2_ = bf16[1024,1024]{1,0:T(8,128)(2,1)} custom-call(f32[256,1024]{1,0:T(8,128)} %copy-done.21, bf16[256,1024]{1,0:T(8,128)(2,1)} %collective-permute-done.19.rest_0_, bf16[256,1024]{1,0:T(8,128)(2,1)} %collective-permute-done.20.rest_1_, bf16[1024,1024]{1,0:T(8,128)(2,1)} %gather_up.5.rest_2_), custom_call_target="tpu_custom_call", output_to_operand_aliasing={{}: (3, {})} | custom-call | flops 1 | bytes 1 | tf_op jit(solution)/shard_map/f2/gather_up/pallas_call | solution.py:141
  176.4 8.9 %collective-permute-done.15.rest_1_ = bf16[256,1024]{1,0:T(8,128)(2,1)} collective-permute-done((bf16[256,1024]{1,0:T(8,128)(2,1)S(1)}, bf16[256,1024]{1,0:T(8,128)(2,1)}, u32[]{:S(2)}, u32[]{:S(2)}) %collective-permute-start.15) | collective-permute-done | bytes 524320 | tf_op jit(solution)/shard_map/t32/ppermute | solution.py:337
  185.4 2.4 %gather_up.7 = bf16[1024,1024]{1,0:T(8,128)(2,1)} custom-call(f32[256,1024]{1,0:T(8,128)} %copy-done.20, bf16[256,1024]{1,0:T(8,128)(2,1)} %collective-permute-done.14.rest_0_, bf16[256,1024]{1,0:T(8,128)(2,1)} %collective-permute-done.15.rest_1_, bf16[1024,1024]{1,0:T(8,128)(2,1)} %gather_up.6.rest_2_), custom_call_target="tpu_custom_call", output_to_operand_aliasing={{}: (3, {})} | custom-call | flops 1 | bytes 1 | tf_op jit(solution)/shard_map/f3/gather_up/pallas_call | solution.py:141
  (123 shorter events, 32.3 us)
Async XLA Ops:
  0.0 37.1 %collective-permute-start.7 = (bf16[1024,8192]{1,0:T(8,128)(2,1)}, bf16[1024,8192]{1,0:T(8,128)(2,1)}, u32[]{:S(2)}, u32[]{:S(2)}) collective-permute-start(bf16[1024,8192]{1,0:T(8,128)(2,1)} %w_ref.23), channel_id=1, source_target_pairs={{0,1},{1,0},{2,3},{3,2},{4,5},{5,4},{6,7},{7,6},{8,9},{9,8},{10,11... | collective-permute-start | bytes 50331656 | tf_op jit(solution)/shard_map/ppermute | solution.py:301
  1.8 18.7 %collective-permute-start.3 = (bf16[128,1024]{1,0:T(8,128)(2,1)}, bf16[128,1024]{1,0:T(8,128)(2,1)S(1)}, u32[]{:S(2)}, u32[]{:S(2)}) collective-permute-start(bf16[128,1024]{1,0:T(8,128)(2,1)} %constant_dynamic-slice_fusion), channel_id=1, source_target_pairs={{0,8},{8,0},{16,24},{24,16},{1,9},{9,1},{17,25},{25,17},{2,10},{10... | collective-permute-start | bytes 786440 | tf_op jit(solution)/shard_map/ppermute | solution.py:297
  3.3 9.4 %collective-permute-start.4 = (bf16[128,1024]{1,0:T(8,128)(2,1)}, bf16[128,1024]{1,0:T(8,128)(2,1)S(1)}, u32[]{:S(2)}, u32[]{:S(2)}) collective-permute-start(bf16[128,1024]{1,0:T(8,128)(2,1)} %constant_dynamic-slice_fusion), channel_id=1, source_target_pairs={{0,16},{8,24},{16,0},{24,8},{1,17},{9,25},{17,1},{25,9},{2,18},{10... | collective-permute-start | bytes 786440 | tf_op jit(solution)/shard_map/ppermute | solution.py:296
  4.6 12.2 %collective-permute-start = (bf16[128,1024]{1,0:T(8,128)(2,1)}, bf16[128,1024]{1,0:T(8,128)(2,1)S(1)}, u32[]{:S(2)}, u32[]{:S(2)}) collective-permute-start(bf16[128,1024]{1,0:T(8,128)(2,1)} %constant_dynamic-slice_fusion.1), channel_id=1, source_target_pairs={{0,8},{8,0},{16,24},{24,16},{1,9},{9,1},{17,25},{25,17},{2,10},{10... | collective-permute-start | bytes 786440 | tf_op jit(solution)/shard_map/ppermute | solution.py:295
  5.1 15.5 %collective-permute-start.1 = (bf16[128,1024]{1,0:T(8,128)(2,1)}, bf16[128,1024]{1,0:T(8,128)(2,1)S(1)}, u32[]{:S(2)}, u32[]{:S(2)}) collective-permute-start(bf16[128,1024]{1,0:T(8,128)(2,1)} %constant_dynamic-slice_fusion.1), channel_id=1, source_target_pairs={{0,16},{8,24},{16,0},{24,8},{1,17},{9,25},{17,1},{25,9},{2,18},{10... | collective-permute-start | bytes 786440 | tf_op jit(solution)/shard_map/ppermute | solution.py:298
  12.7 9.1 %collective-permute-start.5 = (bf16[128,1024]{1,0:T(8,128)(2,1)S(1)}, bf16[128,1024]{1,0:T(8,128)(2,1)S(1)}, u32[]{:S(2)}, u32[]{:S(2)}) collective-permute-start(bf16[128,1024]{1,0:T(8,128)(2,1)S(1)} %collective-permute-done.4), channel_id=1, source_target_pairs={{0,8},{8,0},{16,24},{24,16},{1,9},{9,1},{17,25},{25,17},{2,10},{10... | collective-permute-start | bytes 786440 | tf_op jit(solution)/shard_map/ppermute | solution.py:300
  16.8 7.3 %collective-permute-start.2 = (bf16[128,1024]{1,0:T(8,128)(2,1)S(1)}, bf16[128,1024]{1,0:T(8,128)(2,1)}, u32[]{:S(2)}, u32[]{:S(2)}) collective-permute-start(bf16[128,1024]{1,0:T(8,128)(2,1)S(1)} %collective-permute-done), channel_id=1, source_target_pairs={{0,16},{8,24},{16,0},{24,8},{1,17},{9,25},{17,1},{25,9},{2,18},{10... | collective-permute-start | bytes 786440 | tf_op jit(solution)/shard_map/ppermute | solution.py:299
  35.1 33.3 %copy-start.6 = (bf16[256,1024]{1,0:T(8,128)(2,1)}, bf16[256,1024]{1,0:T(8,128)(2,1)S(1)}, u32[]{:S(2)}) copy-start(bf16[256,1024]{1,0:T(8,128)(2,1)S(1)} %get-tuple-element.26.own_ref.refs_1_) | copy-start | bytes 1572868
  35.1 38.6 %copy-start.2 = (bf16[256,1024]{1,0:T(8,128)(2,1)}, bf16[256,1024]{1,0:T(8,128)(2,1)S(1)}, u32[]{:S(2)}) copy-start(bf16[256,1024]{1,0:T(8,128)(2,1)S(1)} %get-tuple-element.25.refs_0_.own_ref) | copy-start | bytes 1572868
  35.1 2.0 %collective-permute-start.8 = (bf16[256,1024]{1,0:T(8,128)(2,1)S(1)}, bf16[256,1024]{1,0:T(8,128)(2,1)S(1)}, u32[]{:S(2)}, u32[]{:S(2)}) collective-permute-start(bf16[256,1024]{1,0:T(8,128)(2,1)S(1)} %get-tuple-element.25.refs_0_.own_ref), channel_id=1, source_target_pairs={{0,1},{1,0},{2,3},{3,2},{4,5},{5,4},{6,7},{7,6},{8,9},{9,8},{10,11... | collective-permute-start | bytes 1572872 | tf_op jit(solution)/shard_map/a0/ppermute | solution.py:317
  35.2 5.6 %collective-permute-start.6 = (bf16[256,1024]{1,0:T(8,128)(2,1)S(1)}, bf16[256,1024]{1,0:T(8,128)(2,1)S(1)}, u32[]{:S(2)}, u32[]{:S(2)}) collective-permute-start(bf16[256,1024]{1,0:T(8,128)(2,1)S(1)} %get-tuple-element.26.own_ref.refs_1_), channel_id=1, source_target_pairs={{0,1},{1,0},{2,3},{3,2},{4,5},{5,4},{6,7},{7,6},{8,9},{9,8},{10,11... | collective-permute-start | bytes 1572872 | tf_op jit(solution)/shard_map/a0/ppermute | solution.py:317
  37.1 36.6 %copy-start.4 = (bf16[256,1024]{1,0:T(8,128)(2,1)}, bf16[256,1024]{1,0:T(8,128)(2,1)S(1)}, u32[]{:S(2)}) copy-start(bf16[256,1024]{1,0:T(8,128)(2,1)S(1)} %collective-permute-done.8.refs_4_.other_ref) | copy-start | bytes 1572868
  40.0 15.9 %collective-permute-start.16 = (bf16[256,2048]{1,0:T(8,128)(2,1)S(1)}, bf16[256,2048]{1,0:T(8,128)(2,1)S(1)}, u32[]{:S(2)}, u32[]{:S(2)}) collective-permute-start(bf16[256,2048]{1,0:T(8,128)(2,1)S(1)} %unit.16), channel_id=1, source_target_pairs={{0,2},{7,5},{8,10},{15,13},{16,18},{23,21},{24,26},{31,29}} | collective-permute-start | bytes 3145736 | tf_op jit(solution)/shard_map/t00/ppermute | solution.py:337
  43.7 19.1 %collective-permute-start.11 = (bf16[256,2048]{1,0:T(8,128)(2,1)S(1)}, bf16[256,2048]{1,0:T(8,128)(2,1)S(1)}, u32[]{:S(2)}, u32[]{:S(2)}) collective-permute-start(bf16[256,2048]{1,0:T(8,128)(2,1)S(1)} %unit.12), channel_id=1, source_target_pairs={{0,2},{7,5},{8,10},{15,13},{16,18},{23,21},{24,26},{31,29}} | collective-permute-start | bytes 3145736 | tf_op jit(solution)/shard_map/t10/ppermute | solution.py:337
  54.5 2.9 %collective-permute-start.9 = (bf16[256,1024]{1,0:T(8,128)(2,1)S(1)}, bf16[256,1024]{1,0:T(8,128)(2,1)S(1)}, u32[]{:S(2)}, u32[]{:S(2)}) collective-permute-start(bf16[256,1024]{1,0:T(8,128)(2,1)S(1)} %get-tuple-element.28.refs_2_.own_ref), channel_id=1, source_target_pairs={{0,1},{1,0},{2,3},{3,2},{4,5},{5,4},{6,7},{7,6},{8,9},{9,8},{10,11... | collective-permute-start | bytes 1572872 | tf_op jit(solution)/shard_map/a2/ppermute | solution.py:317
  55.8 7.1 %collective-permute-start.10 = (bf16[256,1024]{1,0:T(8,128)(2,1)S(1)}, bf16[256,1024]{1,0:T(8,128)(2,1)S(1)}, u32[]{:S(2)}, u32[]{:S(2)}) collective-permute-start(bf16[256,1024]{1,0:T(8,128)(2,1)S(1)} %get-tuple-element.29.refs_3_.own_ref), channel_id=1, source_target_pairs={{0,1},{1,0},{2,3},{3,2},{4,5},{5,4},{6,7},{7,6},{8,9},{9,8},{10,11... | collective-permute-start | bytes 1572872 | tf_op jit(solution)/shard_map/a2/ppermute | solution.py:317
  61.2 17.8 %collective-permute-start.17 = (bf16[256,2048]{1,0:T(8,128)(2,1)}, bf16[256,2048]{1,0:T(8,128)(2,1)}, u32[]{:S(2)}, u32[]{:S(2)}) collective-permute-start(bf16[256,2048]{1,0:T(8,128)(2,1)} %unit.17), channel_id=1, source_target_pairs={{0,2},{7,5},{8,10},{15,13},{16,18},{23,21},{24,26},{31,29}} | collective-permute-start | bytes 3145736 | tf_op jit(solution)/shard_map/t20/ppermute | solution.py:337
  66.6 17.8 %collective-permute-start.12 = (bf16[256,2048]{1,0:T(8,128)(2,1)}, bf16[256,2048]{1,0:T(8,128)(2,1)}, u32[]{:S(2)}, u32[]{:S(2)}) collective-permute-start(bf16[256,2048]{1,0:T(8,128)(2,1)} %unit.13), channel_id=1, source_target_pairs={{0,2},{7,5},{8,10},{15,13},{16,18},{23,21},{24,26},{31,29}} | collective-permute-start | bytes 3145736 | tf_op jit(solution)/shard_map/t30/ppermute | solution.py:337
  72.2 28.2 %collective-permute-start.21 = (bf16[256,2048]{1,0:T(8,128)(2,1)}, bf16[256,2048]{1,0:T(8,128)(2,1)}, u32[]{:S(2)}, u32[]{:S(2)}) collective-permute-start(bf16[256,2048]{1,0:T(8,128)(2,1)} %unit.20), channel_id=1, source_target_pairs={{0,2},{7,5},{2,4},{5,3},{8,10},{15,13},{10,12},{13,11},{16,18},{23... | collective-permute-start | bytes 3145736 | tf_op jit(solution)/shard_map/t11/ppermute | solution.py:337
  77.5 35.8 %collective-permute-start.24 = (bf16[256,2048]{1,0:T(8,128)(2,1)}, bf16[256,2048]{1,0:T(8,128)(2,1)}, u32[]{:S(2)}, u32[]{:S(2)}) collective-permute-start(bf16[256,2048]{1,0:T(8,128)(2,1)} %unit.22), channel_id=1, source_target_pairs={{0,2},{7,5},{2,4},{5,3},{8,10},{15,13},{10,12},{13,11},{16,18},{23... | collective-permute-start | bytes 3145736 | tf_op jit(solution)/shard_map/t01/ppermute | solution.py:337
  82.9 59.6 %collective-permute-start.18 = (bf16[256,2048]{1,0:T(8,128)(2,1)}, bf16[256,2048]{1,0:T(8,128)(2,1)}, u32[]{:S(2)}, u32[]{:S(2)}) collective-permute-start(bf16[256,2048]{1,0:T(8,128)(2,1)} %unit.18), channel_id=1, source_target_pairs={{0,2},{7,5},{2,4},{5,3},{8,10},{15,13},{10,12},{13,11},{16,18},{23... | collective-permute-start | bytes 3145736 | tf_op jit(solution)/shard_map/t21/ppermute | solution.py:337
  87.5 62.7 %collective-permute-start.13 = (bf16[256,2048]{1,0:T(8,128)(2,1)S(1)}, bf16[256,2048]{1,0:T(8,128)(2,1)}, u32[]{:S(2)}, u32[]{:S(2)}) collective-permute-start(bf16[256,2048]{1,0:T(8,128)(2,1)S(1)} %unit.14), channel_id=1, source_target_pairs={{0,2},{7,5},{2,4},{5,3},{8,10},{15,13},{10,12},{13,11},{16,18},{23... | collective-permute-start | bytes 3145736 | tf_op jit(solution)/shard_map/t31/ppermute | solution.py:337
  106.1 38.5 %copy-start.13 = (bf16[256,1024]{1,0:T(8,128)(2,1)S(1)}, bf16[256,1024]{1,0:T(8,128)(2,1)}, u32[]{:S(2)}) copy-start(bf16[256,1024]{1,0:T(8,128)(2,1)} %copy-done.12) | copy-start | bytes 1572868
  106.1 38.5 %copy-start.19 = (bf16[256,1024]{1,0:T(8,128)(2,1)S(1)}, bf16[256,1024]{1,0:T(8,128)(2,1)}, u32[]{:S(2)}) copy-start(bf16[256,1024]{1,0:T(8,128)(2,1)} %copy-done.17) | copy-start | bytes 1572868
  106.1 51.6 %collective-permute-start.22 = (bf16[256,1024]{1,0:T(8,128)(2,1)S(1)}, bf16[256,1024]{1,0:T(8,128)(2,1)S(1)}, u32[]{:S(2)}, u32[]{:S(2)}) collective-permute-start(bf16[256,1024]{1,0:T(8,128)(2,1)S(1)} %get-tuple-element.39), channel_id=1, source_target_pairs={{0,2},{7,5},{2,4},{5,3},{4,6},{3,1},{8,10},{15,13},{10,12},{13,11}... | collective-permute-start | bytes 1572872 | tf_op jit(solution)/shard_map/t12/ppermute | solution.py:337
  118.9 42.6 %collective-permute-start.25 = (bf16[256,1024]{1,0:T(8,128)(2,1)S(1)}, bf16[256,1024]{1,0:T(8,128)(2,1)S(1)}, u32[]{:S(2)}, u32[]{:S(2)}) collective-permute-start(bf16[256,1024]{1,0:T(8,128)(2,1)S(1)} %get-tuple-element.43), channel_id=1, source_target_pairs={{0,2},{7,5},{2,4},{5,3},{4,6},{3,1},{8,10},{15,13},{10,12},{13,11}... | collective-permute-start | bytes 1572872 | tf_op jit(solution)/shard_map/t02/ppermute | solution.py:337
  120.8 42.7 %collective-permute-start.26 = (bf16[256,1024]{1,0:T(8,128)(2,1)S(1)}, bf16[256,1024]{1,0:T(8,128)(2,1)S(1)}, u32[]{:S(2)}, u32[]{:S(2)}) collective-permute-start(bf16[256,1024]{1,0:T(8,128)(2,1)S(1)} %get-tuple-element.44), channel_id=1, source_target_pairs={{0,3},{7,4},{2,5},{5,2},{4,7},{3,0},{8,11},{15,12},{10,13},{13,10}... | collective-permute-start | bytes 1572872 | tf_op jit(solution)/shard_map/t02/ppermute | solution.py:337
  142.6 28.3 %collective-permute-start.23 = (bf16[256,1024]{1,0:T(8,128)(2,1)S(1)}, bf16[256,1024]{1,0:T(8,128)(2,1)}, u32[]{:S(2)}, u32[]{:S(2)}) collective-permute-start(bf16[256,1024]{1,0:T(8,128)(2,1)S(1)} %get-tuple-element.40), channel_id=1, source_target_pairs={{0,3},{7,4},{2,5},{5,2},{4,7},{3,0},{8,11},{15,12},{10,13},{13,10}... | collective-permute-start | bytes 1572872 | tf_op jit(solution)/shard_map/t12/ppermute | solution.py:337
  150.2 23.0 %collective-permute-start.19 = (bf16[256,1024]{1,0:T(8,128)(2,1)S(1)}, bf16[256,1024]{1,0:T(8,128)(2,1)}, u32[]{:S(2)}, u32[]{:S(2)}) collective-permute-start(bf16[256,1024]{1,0:T(8,128)(2,1)S(1)} %get-tuple-element.36), channel_id=1, source_target_pairs={{0,2},{7,5},{2,4},{5,3},{4,6},{3,1},{8,10},{15,13},{10,12},{13,11}... | collective-permute-start | bytes 1572872 | tf_op jit(solution)/shard_map/t22/ppermute | solution.py:337
  157.7 16.4 %collective-permute-start.20 = (bf16[256,1024]{1,0:T(8,128)(2,1)S(1)}, bf16[256,1024]{1,0:T(8,128)(2,1)}, u32[]{:S(2)}, u32[]{:S(2)}) collective-permute-start(bf16[256,1024]{1,0:T(8,128)(2,1)S(1)} %get-tuple-element.37), channel_id=1, source_target_pairs={{0,3},{7,4},{2,5},{5,2},{4,7},{3,0},{8,11},{15,12},{10,13},{13,10}... | collective-permute-start | bytes 1572872 | tf_op jit(solution)/shard_map/t22/ppermute | solution.py:337
  161.5 14.9 %collective-permute-start.14 = (bf16[256,1024]{1,0:T(8,128)(2,1)S(1)}, bf16[256,1024]{1,0:T(8,128)(2,1)}, u32[]{:S(2)}, u32[]{:S(2)}) collective-permute-start(bf16[256,1024]{1,0:T(8,128)(2,1)S(1)} %get-tuple-element.32), channel_id=1, source_target_pairs={{0,2},{7,5},{2,4},{5,3},{4,6},{3,1},{8,10},{15,13},{10,12},{13,11}... | collective-permute-start | bytes 1572872 | tf_op jit(solution)/shard_map/t32/ppermute | solution.py:337
  164.3 21.1 %collective-permute-start.15 = (bf16[256,1024]{1,0:T(8,128)(2,1)S(1)}, bf16[256,1024]{1,0:T(8,128)(2,1)}, u32[]{:S(2)}, u32[]{:S(2)}) collective-permute-start(bf16[256,1024]{1,0:T(8,128)(2,1)S(1)} %get-tuple-element.33), channel_id=1, source_target_pairs={{0,3},{7,4},{2,5},{5,2},{4,7},{3,0},{8,11},{15,12},{10,13},{13,10}... | collective-permute-start | bytes 1572872 | tf_op jit(solution)/shard_map/t32/ppermute | solution.py:337
  (29 other events, 239.2 us)
